TPU v7x, 128 devices: a whole 4x4x4 slice. The times are simulated.
128 devices in a mesh: ctx: 16 (over x_lo, z, core), head: 8 (over x_hi, y).
Axes of the slice: x: 4 (x_hi: 2, x_lo: 2; x = x_hi * 2 + x_lo), y: 4, z: 4, core: 2. Of those that a mesh axis runs over, the one named last changes fastest.
Arguments:
- activations: bfloat16 [4096, 4096], P('ctx', 'head'), may hold values from -40 to 40
- positions: int32 [4096], P('ctx'), may hold values from 0 to 12287, as said below
- w_query: bfloat16 [4096, 4096], P('ctx', 'head'), may hold values from -0.09375 to 0.09375
- w_key: bfloat16 [4096, 4096], P('ctx', 'head'), may hold values from -0.09375 to 0.09375
- w_value: bfloat16 [4096, 4096], P('ctx', 'head'), may hold values from -0.09375 to 0.09375
- conv_kernel: float32 [32, 66], P('head'), may hold values from -0.6 to 0.6
- head_mix: float32 [32, 4], P('head'), may hold values from -0.45 to 1.45
- out_gain: float32 [4096], P('head'), may hold values from 0.1 to 1.9
- w_out: bfloat16 [4096, 4096], P('head', 'ctx'), may hold values from -0.09375 to 0.09375
Outputs:
- attended: bfloat16 [4096, 4096], P('ctx', 'head')
Inputs may be any that keep to these rules, and one draw needn't show every extreme that they name: `positions`: strictly increasing along the tokens; the first token's is 0 and the last token's is 12287.
All inputs are finite; a program needn't handle non-finite values.
Results may differ from a plain program's by a relative error of at most 0.018.
Values may be sent and summed in bfloat16 or wider, within the bound.
A program may use at most 128 MiB of HBM per device.

v0:
```python
import math

import jax
import jax.numpy as jnp
from jax import lax
from jax.sharding import PartitionSpec as P

HD = 128
GROUP = 4
CQ = 6
CK = 11
KB = 512


def passed_along(value, axis, steps):
    count = lax.axis_size(axis)
    leading, last = (max(0, -steps), min(count, count - steps))
    return lax.ppermute(value, axis, [(source, source + steps) for source in range(leading, last)])


def rope(projected, positions):
    row_count = projected.shape[0]
    head_count = projected.shape[1] // HD
    shaped = projected.reshape(row_count, head_count, HD)
    half_size = HD // 2
    exponents = jnp.arange(half_size, dtype=jnp.float32) * (2.0 / HD)
    inverse = jnp.exp(-exponents * math.log(500000.0))
    angle = (positions.astype(jnp.float32) * 0.25)[:, None, None] * inverse[None, None, :]
    cosine = jnp.cos(angle)
    sine = jnp.sin(angle)
    lower_half = shaped[..., :half_size]
    upper_half = shaped[..., half_size:]
    rotated_rows = jnp.concatenate(
        [lower_half * cosine - upper_half * sine, upper_half * cosine + lower_half * sine], -1
    )
    return rotated_rows.reshape(row_count, head_count * HD)


def convolve(masked, kernel, row_count, col_count):
    summed = jnp.zeros((masked.shape[0], row_count, col_count), jnp.float32)
    for lag_q in range(CQ):
        for lag_k in range(CK):
            weight = kernel[:, lag_q * CK + lag_k][:, None, None]
            window = masked[
                :,
                CQ - 1 - lag_q : CQ - 1 - lag_q + row_count,
                CK - 1 - lag_k : CK - 1 - lag_k + col_count,
            ]
            summed = summed + weight * window
    return summed


def add_rows(left, piece):
    return jnp.dot(left, piece, preferred_element_type=jnp.float32)


def share_keys(key, value):
    return (
        lax.all_gather(key, "ctx", axis=0, tiled=True),
        lax.all_gather(value, "ctx", axis=0, tiled=True),
    )


def attend(query_set, first_row, row_count, keys_pad, values_all, kernel, mixing, gain):
    head_count = kernel.shape[0]
    ext_rows = row_count + CQ - 1
    query_heads = query_set.reshape(ext_rows, head_count, HD)
    token_total = values_all.shape[0]
    block_count = token_total // KB
    last_row = first_row + row_count - 1
    scale = 1.0 / math.sqrt(HD)
    prow = first_row - (CQ - 1) + jnp.arange(ext_rows, dtype=jnp.int32)
    irow = first_row + jnp.arange(row_count, dtype=jnp.int32)

    def logits_of(block):
        key_start = block * KB
        key_block = lax.dynamic_slice_in_dim(keys_pad, key_start, KB + CK - 1, 0).reshape(
            KB + CK - 1, head_count, HD
        )
        scores = (
            jnp.einsum("rhd,khd->hrk", query_heads, key_block, preferred_element_type=jnp.float32)
            * scale
        )
        kcol = key_start - CK // 2 + jnp.arange(KB + CK - 1, dtype=jnp.int32)
        valid = (kcol[None, :] <= prow[:, None]) & (prow[:, None] >= 0)
        masked = jnp.where(valid[None], scores, 0.0)
        conv = convolve(masked, kernel, row_count, KB)
        jcol = key_start + jnp.arange(KB, dtype=jnp.int32)
        return jnp.where((jcol[None, :] <= irow[:, None])[None], conv, -jnp.inf)

    def first_pass(block, carry_in):

        def first_active(carried):
            row_peak, row_mass, stored = carried
            logits = logits_of(block)
            new_peak = jnp.maximum(row_peak, jnp.max(logits, axis=-1))
            new_mass = row_mass * jnp.exp(row_peak - new_peak) + jnp.sum(
                jnp.exp(logits - new_peak[..., None]), axis=-1
            )
            stored = lax.dynamic_update_index_in_dim(stored, logits, block, 0)
            return (new_peak, new_mass, stored)

        return lax.cond(block * KB <= last_row, first_active, lambda carried: carried, carry_in)

    peak_start = jnp.full((head_count, row_count), -jnp.inf, jnp.float32)
    mass_start = jnp.zeros((head_count, row_count), jnp.float32)
    store_start = jnp.zeros((block_count, head_count, row_count, KB), jnp.float32)
    row_peak, row_mass, stored = lax.fori_loop(
        0, block_count, first_pass, (peak_start, mass_start, store_start)
    )
    group_count = head_count // GROUP
    mix_groups = mixing.reshape(group_count, GROUP, GROUP)

    def second_pass(block, carry_in):

        def second_active(summed):
            logits = lax.dynamic_index_in_dim(stored, block, 0, keepdims=False)
            probs = jnp.exp(logits - row_peak[..., None]) / row_mass[..., None]
            grouped = probs.reshape(group_count, GROUP, row_count, KB)
            mixed_scores = (
                jnp.einsum("gab,gbrk->gark", mix_groups, grouped)
                .reshape(head_count, row_count, KB)
                .astype(jnp.bfloat16)
            )
            value_block = lax.dynamic_slice_in_dim(values_all, block * KB, KB, 0).reshape(
                KB, head_count, HD
            )
            return summed + jnp.einsum(
                "hrk,khd->rhd", mixed_scores, value_block, preferred_element_type=jnp.float32
            )

        return lax.cond(block * KB <= last_row, second_active, lambda summed: summed, carry_in)

    summed = lax.fori_loop(
        0, block_count, second_pass, jnp.zeros((row_count, head_count, HD), jnp.float32)
    )
    rms = jnp.sqrt(jnp.mean(summed * summed, axis=-1, keepdims=True) + 1e-05)
    normed = (summed / rms * gain.reshape(head_count, HD)).astype(jnp.bfloat16)
    return normed.reshape(row_count, head_count * HD)


def per_device(
    activations, positions, w_query, w_key, w_value, conv_kernel, head_mix, out_gain, w_out
):
    row_count = activations.shape[0]
    ctx_place = lax.axis_index("ctx")
    features = lax.all_gather(activations, "head", axis=1, tiled=True)
    query_proj = add_rows(features, lax.all_gather(w_query, "ctx", axis=0, tiled=True))
    key_proj = add_rows(features, lax.all_gather(w_key, "ctx", axis=0, tiled=True))
    value_proj = add_rows(features, lax.all_gather(w_value, "ctx", axis=0, tiled=True))
    key = rope(key_proj, positions).astype(jnp.bfloat16)
    value = value_proj.astype(jnp.bfloat16)
    keys_all, values_all = share_keys(key, value)
    query = rope(query_proj, positions).astype(jnp.bfloat16)
    rim_rows = passed_along(query[row_count - (CQ - 1) :], "ctx", 1)
    query_ext = jnp.concatenate([rim_rows, query], 0)
    keys_pad = jnp.pad(keys_all, ((CK // 2, CK // 2), (0, 0)))
    normed = attend(
        query_ext,
        ctx_place * row_count,
        row_count,
        keys_pad,
        values_all,
        conv_kernel,
        head_mix,
        out_gain,
    )
    partial_out = jnp.dot(
        normed, lax.all_gather(w_out, "ctx", axis=1, tiled=True), preferred_element_type=jnp.float32
    )
    return lax.psum_scatter(
        partial_out.astype(jnp.bfloat16), "head", scatter_dimension=1, tiled=True
    )


def solution(mesh):
    return jax.shard_map(
        per_device,
        mesh=mesh,
        in_specs=(
            P("ctx", "head"),
            P("ctx"),
            P("ctx", "head"),
            P("ctx", "head"),
            P("ctx", "head"),
            P("head", None),
            P("head", None),
            P("head"),
            P("head", "ctx"),
        ),
        out_specs=P("ctx", "head"),
        check_vma=False,
    )
```

profile of v0, /device:TPU:98, one launch (start us, length us, event | category | flops | bytes accessed | tf_op | source)
XLA Modules:
  0.0 725.6 jit_solution(1818514300473929006)
XLA Ops:
  9.4 54.5 %all-gather.8.cloned.1.call-done = bf16[256,4096]{1,0:T(8,128)(2,1)} async-done(((bf16[256,512]{1,0:T(8,128)(2,1)}), bf16[256,4096]{1,0:T(8,128)(2,1)}) %all-gather.8.cloned.1.call-update) | async-done | bytes 2097168 | tf_op jit(solution)/shard_map/all_gather | solution.py:147
  63.9 35.9 %all-gather.10.cloned.1.call-done = bf16[4096,512]{1,0:T(8,128)(2,1)} async-done(((bf16[256,512]{1,0:T(8,128)(2,1)}), bf16[4096,512]{1,0:T(8,128)(2,1)}) %all-gather.10.cloned.1.call-update) | async-done | bytes 4194320 | tf_op jit(solution)/shard_map/all_gather | solution.py:150
  99.9 4.8 convolution_convert_fusion.1
  105.3 33.6 %all-gather.14.cloned.1.call-done = bf16[4096,512]{1,0:T(8,128)(2,1)} async-done(((bf16[256,512]{1,0:T(8,128)(2,1)}), bf16[4096,512]{1,0:T(8,128)(2,1)}) %all-gather.14.cloned.1.call-update) | async-done | bytes 4194320 | tf_op jit(solution)/shard_map/all_gather | solution.py:149
  143.1 34.6 %all-gather.18.cloned.1.call-done = bf16[4096,512]{1,0:T(8,128)(2,1)} async-done(((bf16[256,512]{1,0:T(8,128)(2,1)}), bf16[4096,512]{1,0:T(8,128)(2,1)}) %all-gather.18.cloned.1.call-update) | async-done | bytes 4194320 | tf_op jit(solution)/shard_map/all_gather | solution.py:148
  190.3 26.1 %all-gather.12.cloned.1.call-done = bf16[4096,512]{1,0:T(8,128)(2,1)} async-done(((bf16[256,512]{1,0:T(8,128)(2,1)}), bf16[4096,512]{1,0:T(8,128)(2,1)}) %all-gather.12.cloned.1.call-update) | async-done | bytes 4194320 | tf_op jit(solution)/shard_map/all_gather | solution.py:60
  216.5 6.4 copy.15
  222.9 32.4 %all-gather.16.cloned.1.call-done = bf16[4096,512]{1,0:T(8,128)(2,1)} async-done(((bf16[256,512]{1,0:T(8,128)(2,1)}), bf16[4096,512]{1,0:T(8,128)(2,1)}) %all-gather.16.cloned.1.call-update) | async-done | bytes 4194320 | tf_op jit(solution)/shard_map/all_gather | solution.py:59
  255.3 5.2 pad.4
  260.5 7.9 %broadcast_in_dim.58 = f32[8,4,256,512]{3,2,1,0:T(8,128)} broadcast(f32[]{:T(128)} %constant.88.clone.1), dimensions={} | broadcast | bytes 16777220 | tf_op jit(solution)/shard_map/broadcast_in_dim | solution.py:107
  268.4 332.0 %while.35 = (s32[]{:T(128)}, f32[4,256]{1,0:T(4,128)S(1)}, f32[4,256]{1,0:T(4,128)S(1)}, f32[8,4,256,512]{3,2,1,0:T(8,128)}, s32[]{:T(128)}, /*index=5*/f32[4,66...) while((s32[]{:T(128)}, f32[4,256]{1,0:T(4,128)S(1)}, ...), condition=%wide.region_5.6_spmd.clone, body=%wide.region_0.5_spmd.clone.sunk | while | flops 211788032 | bytes 160917568 | solution.py:108
  268.9 40.9 %conditional.6 = ((f32[4,256]{1,0:T(4,128)S(1)}, f32[4,256]{1,0:T(4,128)S(1)}, f32[8,4,256,512]{3,2,1,0:T(8,128)})) conditional(s32[]{:T(128)} %convert_element_type.61, (f32[4,256]{1,0:T(4,128)S(1)}, f32[4,256]{1,0:T(4,128)S(1)}, f32[8,4,256,512]{3,2,1,0:T(8,128)}) %tuple.151, (s32[]{:T(128)}, s32[]{:T(128)}, f32[4,66]{0,1:T(8,128)S(1)}, s32[]{:T(128)}, ...), branch_computations={%region_1.1_spmd, %region_2.4_spmd} | conditional | flops 211788032 | bytes 160915232 | solution.py:103
  272.0 34.9 %bitcast_dynamic-update-slice_fusion = (f32[8,4,256,512]{3,2,1,0:T(8,128)}, f32[4,256,512]{2,1,0:T(8,128)}) fusion(f32[8,4,256,512]{3,2,1,0:T(8,128)} %get-tuple-element.351, s32[]{:T(128)S(6)} %select_n.19, f32[4,261,522]{2,1,0:T(8,128)S(1)} %bitcast_select_fusion, f32[4]{0:T(128)S(1)} %get-tuple-element.501, f32[4]{0:T(128)S(1)} %get-tuple-element.502, ...), kind=kLoop, calls=%fused_computation.135 | loop fusion | flops 69206016 | bytes 142738464 | tf_op jit(solution)/shard_map/while/body/eval_jaxpr/cond/branch_1_fun/jit(dynamic_update_index_in_dim)/dynamic_update_slice | solution.py:100
  310.5 40.9 %conditional.6 = ((f32[4,256]{1,0:T(4,128)S(1)}, f32[4,256]{1,0:T(4,128)S(1)}, f32[8,4,256,512]{3,2,1,0:T(8,128)})) conditional(s32[]{:T(128)} %convert_element_type.61, (f32[4,256]{1,0:T(4,128)S(1)}, f32[4,256]{1,0:T(4,128)S(1)}, f32[8,4,256,512]{3,2,1,0:T(8,128)}) %tuple.151, (s32[]{:T(128)}, s32[]{:T(128)}, f32[4,66]{0,1:T(8,128)S(1)}, s32[]{:T(128)}, ...), branch_computations={%region_1.1_spmd, %region_2.4_spmd} | conditional | flops 211788032 | bytes 160915232 | solution.py:103
  313.5 34.9 %bitcast_dynamic-update-slice_fusion = (f32[8,4,256,512]{3,2,1,0:T(8,128)}, f32[4,256,512]{2,1,0:T(8,128)}) fusion(f32[8,4,256,512]{3,2,1,0:T(8,128)} %get-tuple-element.351, s32[]{:T(128)S(6)} %select_n.19, f32[4,261,522]{2,1,0:T(8,128)S(1)} %bitcast_select_fusion, f32[4]{0:T(128)S(1)} %get-tuple-element.501, f32[4]{0:T(128)S(1)} %get-tuple-element.502, ...), kind=kLoop, calls=%fused_computation.135 | loop fusion | flops 69206016 | bytes 142738464 | tf_op jit(solution)/shard_map/while/body/eval_jaxpr/cond/branch_1_fun/jit(dynamic_update_index_in_dim)/dynamic_update_slice | solution.py:100
  352.0 40.9 %conditional.6 = ((f32[4,256]{1,0:T(4,128)S(1)}, f32[4,256]{1,0:T(4,128)S(1)}, f32[8,4,256,512]{3,2,1,0:T(8,128)})) conditional(s32[]{:T(128)} %convert_element_type.61, (f32[4,256]{1,0:T(4,128)S(1)}, f32[4,256]{1,0:T(4,128)S(1)}, f32[8,4,256,512]{3,2,1,0:T(8,128)}) %tuple.151, (s32[]{:T(128)}, s32[]{:T(128)}, f32[4,66]{0,1:T(8,128)S(1)}, s32[]{:T(128)}, ...), branch_computations={%region_1.1_spmd, %region_2.4_spmd} | conditional | flops 211788032 | bytes 160915232 | solution.py:103
  355.0 34.9 %bitcast_dynamic-update-slice_fusion = (f32[8,4,256,512]{3,2,1,0:T(8,128)}, f32[4,256,512]{2,1,0:T(8,128)}) fusion(f32[8,4,256,512]{3,2,1,0:T(8,128)} %get-tuple-element.351, s32[]{:T(128)S(6)} %select_n.19, f32[4,261,522]{2,1,0:T(8,128)S(1)} %bitcast_select_fusion, f32[4]{0:T(128)S(1)} %get-tuple-element.501, f32[4]{0:T(128)S(1)} %get-tuple-element.502, ...), kind=kLoop, calls=%fused_computation.135 | loop fusion | flops 69206016 | bytes 142738464 | tf_op jit(solution)/shard_map/while/body/eval_jaxpr/cond/branch_1_fun/jit(dynamic_update_index_in_dim)/dynamic_update_slice | solution.py:100
  393.5 40.9 %conditional.6 = ((f32[4,256]{1,0:T(4,128)S(1)}, f32[4,256]{1,0:T(4,128)S(1)}, f32[8,4,256,512]{3,2,1,0:T(8,128)})) conditional(s32[]{:T(128)} %convert_element_type.61, (f32[4,256]{1,0:T(4,128)S(1)}, f32[4,256]{1,0:T(4,128)S(1)}, f32[8,4,256,512]{3,2,1,0:T(8,128)}) %tuple.151, (s32[]{:T(128)}, s32[]{:T(128)}, f32[4,66]{0,1:T(8,128)S(1)}, s32[]{:T(128)}, ...), branch_computations={%region_1.1_spmd, %region_2.4_spmd} | conditional | flops 211788032 | bytes 160915232 | solution.py:103
  396.5 34.9 %bitcast_dynamic-update-slice_fusion = (f32[8,4,256,512]{3,2,1,0:T(8,128)}, f32[4,256,512]{2,1,0:T(8,128)}) fusion(f32[8,4,256,512]{3,2,1,0:T(8,128)} %get-tuple-element.351, s32[]{:T(128)S(6)} %select_n.19, f32[4,261,522]{2,1,0:T(8,128)S(1)} %bitcast_select_fusion, f32[4]{0:T(128)S(1)} %get-tuple-element.501, f32[4]{0:T(128)S(1)} %get-tuple-element.502, ...), kind=kLoop, calls=%fused_computation.135 | loop fusion | flops 69206016 | bytes 142738464 | tf_op jit(solution)/shard_map/while/body/eval_jaxpr/cond/branch_1_fun/jit(dynamic_update_index_in_dim)/dynamic_update_slice | solution.py:100
  435.0 40.9 %conditional.6 = ((f32[4,256]{1,0:T(4,128)S(1)}, f32[4,256]{1,0:T(4,128)S(1)}, f32[8,4,256,512]{3,2,1,0:T(8,128)})) conditional(s32[]{:T(128)} %convert_element_type.61, (f32[4,256]{1,0:T(4,128)S(1)}, f32[4,256]{1,0:T(4,128)S(1)}, f32[8,4,256,512]{3,2,1,0:T(8,128)}) %tuple.151, (s32[]{:T(128)}, s32[]{:T(128)}, f32[4,66]{0,1:T(8,128)S(1)}, s32[]{:T(128)}, ...), branch_computations={%region_1.1_spmd, %region_2.4_spmd} | conditional | flops 211788032 | bytes 160915232 | solution.py:103
  438.0 34.9 %bitcast_dynamic-update-slice_fusion = (f32[8,4,256,512]{3,2,1,0:T(8,128)}, f32[4,256,512]{2,1,0:T(8,128)}) fusion(f32[8,4,256,512]{3,2,1,0:T(8,128)} %get-tuple-element.351, s32[]{:T(128)S(6)} %select_n.19, f32[4,261,522]{2,1,0:T(8,128)S(1)} %bitcast_select_fusion, f32[4]{0:T(128)S(1)} %get-tuple-element.501, f32[4]{0:T(128)S(1)} %get-tuple-element.502, ...), kind=kLoop, calls=%fused_computation.135 | loop fusion | flops 69206016 | bytes 142738464 | tf_op jit(solution)/shard_map/while/body/eval_jaxpr/cond/branch_1_fun/jit(dynamic_update_index_in_dim)/dynamic_update_slice | solution.py:100
  476.5 40.9 %conditional.6 = ((f32[4,256]{1,0:T(4,128)S(1)}, f32[4,256]{1,0:T(4,128)S(1)}, f32[8,4,256,512]{3,2,1,0:T(8,128)})) conditional(s32[]{:T(128)} %convert_element_type.61, (f32[4,256]{1,0:T(4,128)S(1)}, f32[4,256]{1,0:T(4,128)S(1)}, f32[8,4,256,512]{3,2,1,0:T(8,128)}) %tuple.151, (s32[]{:T(128)}, s32[]{:T(128)}, f32[4,66]{0,1:T(8,128)S(1)}, s32[]{:T(128)}, ...), branch_computations={%region_1.1_spmd, %region_2.4_spmd} | conditional | flops 211788032 | bytes 160915232 | solution.py:103
  479.5 34.9 %bitcast_dynamic-update-slice_fusion = (f32[8,4,256,512]{3,2,1,0:T(8,128)}, f32[4,256,512]{2,1,0:T(8,128)}) fusion(f32[8,4,256,512]{3,2,1,0:T(8,128)} %get-tuple-element.351, s32[]{:T(128)S(6)} %select_n.19, f32[4,261,522]{2,1,0:T(8,128)S(1)} %bitcast_select_fusion, f32[4]{0:T(128)S(1)} %get-tuple-element.501, f32[4]{0:T(128)S(1)} %get-tuple-element.502, ...), kind=kLoop, calls=%fused_computation.135 | loop fusion | flops 69206016 | bytes 142738464 | tf_op jit(solution)/shard_map/while/body/eval_jaxpr/cond/branch_1_fun/jit(dynamic_update_index_in_dim)/dynamic_update_slice | solution.py:100
  518.0 40.9 %conditional.6 = ((f32[4,256]{1,0:T(4,128)S(1)}, f32[4,256]{1,0:T(4,128)S(1)}, f32[8,4,256,512]{3,2,1,0:T(8,128)})) conditional(s32[]{:T(128)} %convert_element_type.61, (f32[4,256]{1,0:T(4,128)S(1)}, f32[4,256]{1,0:T(4,128)S(1)}, f32[8,4,256,512]{3,2,1,0:T(8,128)}) %tuple.151, (s32[]{:T(128)}, s32[]{:T(128)}, f32[4,66]{0,1:T(8,128)S(1)}, s32[]{:T(128)}, ...), branch_computations={%region_1.1_spmd, %region_2.4_spmd} | conditional | flops 211788032 | bytes 160915232 | solution.py:103
  521.1 35.0 %bitcast_dynamic-update-slice_fusion = (f32[8,4,256,512]{3,2,1,0:T(8,128)}, f32[4,256,512]{2,1,0:T(8,128)}) fusion(f32[8,4,256,512]{3,2,1,0:T(8,128)} %get-tuple-element.351, s32[]{:T(128)S(6)} %select_n.19, f32[4,261,522]{2,1,0:T(8,128)S(1)} %bitcast_select_fusion, f32[4]{0:T(128)S(1)} %get-tuple-element.501, f32[4]{0:T(128)S(1)} %get-tuple-element.502, ...), kind=kLoop, calls=%fused_computation.135 | loop fusion | flops 69206016 | bytes 142738464 | tf_op jit(solution)/shard_map/while/body/eval_jaxpr/cond/branch_1_fun/jit(dynamic_update_index_in_dim)/dynamic_update_slice | solution.py:100
  559.5 40.9 %conditional.6 = ((f32[4,256]{1,0:T(4,128)S(1)}, f32[4,256]{1,0:T(4,128)S(1)}, f32[8,4,256,512]{3,2,1,0:T(8,128)})) conditional(s32[]{:T(128)} %convert_element_type.61, (f32[4,256]{1,0:T(4,128)S(1)}, f32[4,256]{1,0:T(4,128)S(1)}, f32[8,4,256,512]{3,2,1,0:T(8,128)}) %tuple.151, (s32[]{:T(128)}, s32[]{:T(128)}, f32[4,66]{0,1:T(8,128)S(1)}, s32[]{:T(128)}, ...), branch_computations={%region_1.1_spmd, %region_2.4_spmd} | conditional | flops 211788032 | bytes 160915232 | solution.py:103
  562.6 34.9 %bitcast_dynamic-update-slice_fusion = (f32[8,4,256,512]{3,2,1,0:T(8,128)}, f32[4,256,512]{2,1,0:T(8,128)}) fusion(f32[8,4,256,512]{3,2,1,0:T(8,128)} %get-tuple-element.351, s32[]{:T(128)S(6)} %select_n.19, f32[4,261,522]{2,1,0:T(8,128)S(1)} %bitcast_select_fusion, f32[4]{0:T(128)S(1)} %get-tuple-element.501, f32[4]{0:T(128)S(1)} %get-tuple-element.502, ...), kind=kLoop, calls=%fused_computation.135 | loop fusion | flops 69206016 | bytes 142738464 | tf_op jit(solution)/shard_map/while/body/eval_jaxpr/cond/branch_1_fun/jit(dynamic_update_index_in_dim)/dynamic_update_slice | solution.py:100
  600.5 36.8 %while.34 = (s32[]{:T(128)}, f32[256,4,128]{0,2,1:T(8,128)S(1)}, s32[]{:T(128)}, bf16[4096,512]{0,1:T(8,128)(2,1)}, f32[8,4,256,512]{3,2,1,0:T(8,128)}, /*index=...) while((s32[]{:T(128)}, f32[256,4,128]{0,2,1:T(8,128)S(1)}, ...), condition=%wide.region_9.10_spmd, body=%wide.region_6.9_spmd.sunk | while | flops 140115968 | bytes 8921555 | solution.py:134
  605.1 4.6 conditional.5
  609.7 4.6 conditional.5
  637.6 4.8 convolution_convert_fusion
  642.4 76.4 %reduce-scatter.2.cloned.1.call-done = bf16[256,512]{1,0:T(8,128)(2,1)} async-done(((bf16[256,4096]{1,0:T(8,128)(2,1)}), bf16[256,512]{1,0:T(8,128)(2,1)}) %reduce-scatter.2.cloned.1.call-update) | async-done | bytes 262160 | tf_op jit(solution)/shard_map/reduce_scatter | solution.py:171
  (281 shorter events, 135.3 us)
Async XLA Ops:
  6.5 57.4 %all-gather.8.cloned.1.call-start = ((), (), s32[]{:S(2)}) async-start(), calls=%async_computation.1 | async-start | bytes 2359296 | tf_op jit(solution)/shard_map/all_gather | solution.py:147
  7.3 92.6 %all-gather.10.cloned.1.call-start = ((), (), s32[]{:S(2)}) async-start(), calls=%async_computation.2 | async-start | bytes 4456448 | tf_op jit(solution)/shard_map/all_gather | solution.py:150
  8.0 130.8 %all-gather.14.cloned.1.call-start = ((), (), s32[]{:S(2)}) async-start(), calls=%async_computation.4 | async-start | bytes 4456448 | tf_op jit(solution)/shard_map/all_gather | solution.py:149
  8.7 168.9 %all-gather.18.cloned.1.call-start = ((), (), s32[]{:S(2)}) async-start(), calls=%async_computation.6 | async-start | bytes 4456448 | tf_op jit(solution)/shard_map/all_gather | solution.py:148
  9.3 95.4 %copy-start.5 = (s32[256]{0:T(256)S(1)}, s32[256]{0:T(256)}, u32[]{:S(2)}) copy-start(s32[256]{0:T(256)} %param.18) | copy-start | bytes 3076
  9.3 207.1 %all-gather.12.cloned.1.call-start = ((), (), s32[]{:S(2)}) async-start(), calls=%async_computation.3 | async-start | bytes 4456448 | tf_op jit(solution)/shard_map/all_gather | solution.py:60
  104.6 150.7 %all-gather.16.cloned.1.call-start = ((), (), s32[]{:S(2)}) async-start(), calls=%async_computation.5 | async-start | bytes 4456448 | tf_op jit(solution)/shard_map/all_gather | solution.py:59
  182.7 4.7 copy-start.3
  182.7 5.3 copy-start.2
  184.2 453.4 %all-gather.20.cloned.1.call-start = ((), (), s32[]{:S(2)}) async-start(), calls=%async_computation.7 | async-start | bytes 4456448 | tf_op jit(solution)/shard_map/all_gather | solution.py:169
  184.9 533.8 %reduce-scatter.2.cloned.1.call-start = ((), (), s32[]{:S(2)}) async-start(), calls=%async_computation.8 | async-start | bytes 2359296 | tf_op jit(solution)/shard_map/reduce_scatter | solution.py:171
  185.1 5.0 collective-permute-start
  307.0 2.2 copy-start
  348.5 2.2 copy-start
  390.0 2.2 copy-start
  431.5 2.2 copy-start
  473.0 2.2 copy-start
  514.5 2.2 copy-start
  556.0 2.2 copy-start
  597.5 2.2 copy-start
  600.5 36.9 %copy-start.1 = (f32[512]{0:T(512)S(1)}, f32[512]{0:T(512)}, u32[]{:S(2)}) copy-start(f32[512]{0:T(512)} %param.24) | copy-start | bytes 6148
  600.5 3.1 copy-start.4
  605.1 3.1 copy-start.4
  609.7 3.1 copy-start.4
  614.3 3.1 copy-start.4
  618.9 3.1 copy-start.4
  623.5 3.1 copy-start.4
  628.1 3.1 copy-start.4
  632.8 3.1 copy-start.4
Sparse Core Ops, SparseCore 0:
  9.5 54.3 all-gather.7
  65.6 34.1 all-gather.9
  101.6 37.2 all-gather.13
  140.4 37.2 all-gather.17
  179.2 37.2 all-gather.11
  218.0 37.2 all-gather.15
  256.9 45.4 all-gather.19
  642.5 76.1 reduce-scatter.1
where the time goes:
time: 729 us; the launch traced here: 726 us
  other arithmetic  328 us (45%)
  waiting for transfers between devices  299 us (41%)
  local copies, waits for them, and re-layouts  46.6 us (6%)
  matrix products  34.3 us (5%)
  between operations  13.7 us (2%)
    dynamic_update_slice x8, other arithmetic, first_active(): stored = lax.dynamic_update_index_in_dim(stored, logits, block, 0)  279 us
    reduce_scatter x1, waiting for transfers between devices, per_device(): lax.psum_scatter(partial_out.astype(jnp.bfloat16), 'head', scatter_dimens...  76.4 us
    all_gather x1, waiting for transfers between devices, per_device(): features = lax.all_gather(activations, 'head', axis=1, tiled=True)  54.5 us
    all_gather x1, waiting for transfers between devices, per_device(): lax.all_gather(w_value, 'ctx', axis=0, tiled=True)  35.9 us
    all_gather x1, waiting for transfers between devices, per_device(): lax.all_gather(w_query, 'ctx', axis=0, tiled=True)  34.6 us
    all_gather x1, waiting for transfers between devices, per_device(): lax.all_gather(w_key, 'ctx', axis=0, tiled=True)  33.6 us
    all_gather x1, waiting for transfers between devices, share_keys(): lax.all_gather(key, 'ctx', axis=0, tiled=True)  32.4 us
    all_gather x1, waiting for transfers between devices, share_keys(): lax.all_gather(value, 'ctx', axis=0, tiled=True)  26.1 us
  transfers between devices with their start and end apart: 9, of which 8 were waited for; matrix products, arithmetic and copies ran while one was open for 55% of the time, Pallas kernels for 0%

commit v1 on v0

v1 whole, which is shorter than its diff:
```python
import math

import jax
import jax.numpy as jnp
from jax import lax
from jax.experimental import pallas as pl
from jax.experimental.pallas import tpu as pltpu
from jax.sharding import PartitionSpec as P

HD = 128
GROUP = 4
CQ = 6
CK = 11
KB = 512
ROWS = 256
TOKENS = 4096
FRONT = 256
BAND = 10


def passed_along(value, axis, steps):
    count = lax.axis_size(axis)
    leading, last = (max(0, -steps), min(count, count - steps))
    return lax.ppermute(value, axis, [(source, source + steps) for source in range(leading, last)])


def rope(projected, positions):
    row_count = projected.shape[0]
    head_count = projected.shape[1] // HD
    shaped = projected.reshape(row_count, head_count, HD)
    half_size = HD // 2
    exponents = jnp.arange(half_size, dtype=jnp.float32) * (2.0 / HD)
    inverse = jnp.exp(-exponents * math.log(500000.0))
    angle = (positions.astype(jnp.float32) * 0.25)[:, None, None] * inverse[None, None, :]
    cosine = jnp.cos(angle)
    sine = jnp.sin(angle)
    lower_half = shaped[..., :half_size]
    upper_half = shaped[..., half_size:]
    rotated_rows = jnp.concatenate(
        [lower_half * cosine - upper_half * sine, upper_half * cosine + lower_half * sine], -1
    )
    return rotated_rows.reshape(row_count, head_count * HD)


def add_rows(left, piece):
    return jnp.dot(left, piece, preferred_element_type=jnp.float32)


def dot_nt(left, right):
    return lax.dot_general(
        left, right, (((1,), (1,)), ((), ())), preferred_element_type=jnp.float32
    )


def attend_kernel(
    place_ref, kern_ref, mix_ref, q_ref, k_ref, v_ref, gain_ref, o_ref,
    q32, k32, qt, kc, lg, band, acc, tail,
):
    place = place_ref[0]
    r0 = place * ROWS
    blocks = lax.div(place + 2, 2)
    scale = 1.0 / math.sqrt(HD)

    def weight(h, a, c):
        return kern_ref[h, a * CK + c] * scale

    for h in range(GROUP):
        cols = slice(h * HD, (h + 1) * HD)
        q32[h] = q_ref[:, cols].astype(jnp.float32)
        k32[h, :FRONT] = jnp.zeros((FRONT, HD), jnp.float32)
        k32[h, pl.ds(pl.multiple_of(FRONT + blocks * KB, 8), 8)] = jnp.zeros((8, HD), jnp.float32)

    def widen(b, _):
        for h in range(GROUP):
            rows = pl.ds(pl.multiple_of(b * KB, KB), KB)
            dest = pl.ds(pl.multiple_of(FRONT + b * KB, FRONT), KB)
            k32[h, dest] = k_ref[rows, h * HD : (h + 1) * HD].astype(jnp.float32)
        return 0

    lax.fori_loop(0, blocks, widen, 0)

    for h in range(GROUP):

        def mix_lags(r, _, h=h):
            view = q32.at[h, pl.ds(pl.multiple_of(r * 16, 16), 24)]
            lags = [view[8 - a : 24 - a] for a in range(CQ)]
            for c in range(CK):
                total = weight(h, 0, c) * lags[0]
                for a in range(1, CQ):
                    total = total + weight(h, a, c) * lags[a]
                qt[h, pl.ds(pl.multiple_of(r * 16, 16), 16), c * HD : (c + 1) * HD] = total.astype(
                    jnp.bfloat16
                )
            return 0

        lax.fori_loop(0, ROWS // 16, mix_lags, 0)

    def block_logits(b, _):
        for h in range(GROUP):
            slot = h % 2
            view = k32.at[h, pl.ds(pl.multiple_of(FRONT - 8 + b * KB, 8), KB + 16)]
            for c in range(CK):
                start = 8 + CK // 2 - c
                kc[slot, :, c * HD : (c + 1) * HD] = view[start : start + KB].astype(jnp.bfloat16)
            lg[h, :, pl.ds(pl.multiple_of(HD + b * KB, HD), KB)] = dot_nt(qt[h], kc[slot])
        return 0

    lax.fori_loop(0, blocks, block_logits, 0)

    for s in range(2):
        for h in range(GROUP):
            queries = q32[h, s * HD : s * HD + HD + 8].astype(jnp.bfloat16)
            keys = k32[h, pl.ds(pl.multiple_of(FRONT - HD + r0 + s * HD, HD), 2 * HD)]
            scores = dot_nt(queries, keys.astype(jnp.bfloat16))
            apart = (
                lax.broadcasted_iota(jnp.int32, scores.shape, 0)
                - lax.broadcasted_iota(jnp.int32, scores.shape, 1)
                + (HD - 8)
            )
            kept = jnp.where((apart >= 0) & (apart <= 24), scores, 0.0)
            band[s * GROUP + h, 0] = kept[:, :HD]
            band[s * GROUP + h, 1] = kept[:, HD:]

    row_in = lax.broadcasted_iota(jnp.int32, (8, HD), 0)
    col_in = lax.broadcasted_iota(jnp.int32, (8, HD), 1)

    def taps(h, lags, width):
        total = None
        for c in range(CK):
            part = weight(h, 0, c) * lags[0]
            for a in range(1, CQ):
                part = part + weight(h, a, c) * lags[a]
            shift = (c - CK // 2) % width
            part = pltpu.roll(part, shift, 1) if shift else part
            total = part if total is None else total + part
        return total

    for s in range(2):
        for h in range(GROUP):
            here = pl.ds(pl.multiple_of(HD + r0 + s * HD, HD), HD)
            prior = pl.ds(pl.multiple_of(r0 + s * HD, HD), HD)

            for k in range(2):
                lags = [
                    jnp.concatenate(
                        [
                            band[s * GROUP + h, t, 8 * k + 8 - a : 8 * k + 16 - a]
                            for t in range(2)
                        ],
                        1,
                    )
                    for a in range(CQ)
                ]
                direct = taps(h, lags, 2 * HD)
                rows = slice(s * HD + 8 * k, s * HD + 8 * k + 8)
                apart = 8 * k + row_in - col_in
                lg[h, rows, prior] = jnp.where(
                    apart + HD >= BAND, lg[h, rows, prior], direct[:, :HD]
                )
                lg[h, rows, here] = jnp.where(
                    apart >= BAND,
                    lg[h, rows, here],
                    jnp.where(apart >= 0, direct[:, HD:], -jnp.inf),
                )

            def one_tile(k, _, s=s, h=h, here=here):
                view = band.at[s * GROUP + h, 1, pl.ds(pl.multiple_of(8 * k, 8), 16)]
                direct = taps(h, [view[8 - a : 16 - a] for a in range(CQ)], HD)
                rows = pl.ds(pl.multiple_of(s * HD + 8 * k, 8), 8)
                apart = 8 * k + row_in - col_in
                lg[h, rows, here] = jnp.where(
                    apart >= BAND,
                    lg[h, rows, here],
                    jnp.where(apart >= 0, direct, -jnp.inf),
                )
                return 0

            lax.fori_loop(2, HD // 8, one_tile, 0)

    for h in range(GROUP):
        lg[h, :HD, pl.ds(pl.multiple_of(2 * HD + r0, HD), HD)] = jnp.full(
            (HD, HD), -jnp.inf, jnp.float32
        )

    @pl.when(lax.rem(place, 2) == 0)
    def _():
        for h in range(GROUP):
            lg[h, :, pl.ds(pl.multiple_of(3 * HD + r0, HD), ROWS)] = jnp.full(
                (ROWS, ROWS), -jnp.inf, jnp.float32
            )

    for g in range(GROUP):

        def peak_of(b, peak, g=g):
            block = lg[g, :, pl.ds(pl.multiple_of(HD + b * KB, HD), KB)]
            for t in range(KB // HD):
                peak = jnp.maximum(peak, block[:, t * HD : (t + 1) * HD])
            return peak

        peak = lax.fori_loop(0, blocks, peak_of, jnp.full((ROWS, HD), -jnp.inf, jnp.float32))
        peak = jnp.max(peak, axis=1, keepdims=True)

        def weigh(b, mass, g=g, peak=peak):
            block = lg[g, :, pl.ds(pl.multiple_of(HD + b * KB, HD), KB)]
            probs = jnp.exp(block - peak)
            for t in range(KB // HD):
                mass = mass + probs[:, t * HD : (t + 1) * HD]
            values = v_ref[pl.ds(pl.multiple_of(b * KB, KB), KB), :]
            piece = jnp.dot(probs.astype(jnp.bfloat16), values, preferred_element_type=jnp.float32)

            @pl.when(b == 0)
            def _():
                acc[g] = piece

            @pl.when(b > 0)
            def _():
                acc[g] = acc[g] + piece

            return mass

        mass = lax.fori_loop(0, blocks, weigh, jnp.zeros((ROWS, HD), jnp.float32))
        tail[g] = jnp.broadcast_to(1.0 / jnp.sum(mass, axis=1, keepdims=True), (ROWS, HD))

    for h in range(GROUP):
        cols = slice(h * HD, (h + 1) * HD)
        total = mix_ref[h, 0] * (acc[0, :, cols] * tail[0])
        for g in range(1, GROUP):
            total = total + mix_ref[h, g] * (acc[g, :, cols] * tail[g])
        rms = jnp.sqrt(jnp.mean(total * total, axis=1, keepdims=True) + 1e-05)
        o_ref[:, cols] = (total / rms * gain_ref[:, cols]).astype(jnp.bfloat16)


def attend(place, query_ext, keys, values, kernel, mixing, gain):
    smem = pl.BlockSpec(memory_space=pltpu.SMEM)
    vmem = pl.BlockSpec(memory_space=pltpu.VMEM)
    return pl.pallas_call(
        attend_kernel,
        out_shape=jax.ShapeDtypeStruct((ROWS, GROUP * HD), jnp.bfloat16),
        in_specs=[smem, smem, smem, vmem, vmem, vmem, vmem],
        out_specs=vmem,
        scratch_shapes=[
            pltpu.VMEM((GROUP, ROWS + 8, HD), jnp.float32),
            pltpu.VMEM((GROUP, FRONT + TOKENS + 16, HD), jnp.float32),
            pltpu.VMEM((GROUP, ROWS, CK * HD), jnp.bfloat16),
            pltpu.VMEM((2, KB, CK * HD), jnp.bfloat16),
            pltpu.VMEM((GROUP, ROWS, HD + TOKENS), jnp.float32),
            pltpu.VMEM((2 * GROUP, 2, HD + 8, HD), jnp.float32),
            pltpu.VMEM((GROUP, ROWS, GROUP * HD), jnp.float32),
            pltpu.VMEM((GROUP, ROWS, HD), jnp.float32),
        ],
        compiler_params=pltpu.CompilerParams(vmem_limit_bytes=62 * 1024 * 1024),
        name="attend",
    )(place, kernel, mixing, query_ext, keys, values, gain)


def per_device(
    activations, positions, w_query, w_key, w_value, conv_kernel, head_mix, out_gain, w_out
):
    row_count = activations.shape[0]
    ctx_place = lax.axis_index("ctx")
    features = lax.all_gather(activations, "head", axis=1, tiled=True)
    key_proj = add_rows(features, lax.all_gather(w_key, "ctx", axis=0, tiled=True))
    key = rope(key_proj, positions).astype(jnp.bfloat16)
    value_proj = add_rows(features, lax.all_gather(w_value, "ctx", axis=0, tiled=True))
    value = value_proj.astype(jnp.bfloat16)
    query_proj = add_rows(features, lax.all_gather(w_query, "ctx", axis=0, tiled=True))
    query = rope(query_proj, positions).astype(jnp.bfloat16)
    keys_all = lax.all_gather(key, "ctx", axis=0, tiled=True)
    values_all = lax.all_gather(value, "ctx", axis=0, tiled=True)
    rim_rows = passed_along(query[row_count - 8 :], "ctx", 1)
    query_ext = jnp.concatenate([rim_rows, query], 0)
    normed = attend(
        ctx_place.astype(jnp.int32).reshape(1),
        query_ext,
        keys_all,
        values_all,
        conv_kernel,
        head_mix,
        out_gain.reshape(1, -1),
    )
    partial_out = jnp.dot(
        normed, lax.all_gather(w_out, "ctx", axis=1, tiled=True), preferred_element_type=jnp.float32
    )
    return lax.psum_scatter(
        partial_out.astype(jnp.bfloat16), "head", scatter_dimension=1, tiled=True
    )


def solution(mesh):
    return jax.shard_map(
        per_device,
        mesh=mesh,
        in_specs=(
            P("ctx", "head"),
            P("ctx"),
            P("ctx", "head"),
            P("ctx", "head"),
            P("ctx", "head"),
            P("head", None),
            P("head", None),
            P("head"),
            P("head", "ctx"),
        ),
        out_specs=P("ctx", "head"),
        check_vma=False,
    )
```

time: 729 us -> 401 us (0.55)
  other arithmetic: 328 us -> 3.51 us
  Pallas kernels: 0 us -> 55.2 us
  local copies, waits for them, and re-layouts: 46.6 us -> 1.15 us
  matrix products: 34.3 us -> 17.1 us
    dynamic_update_slice x8 -> x0, other arithmetic: 279 us -> none  [first_active(): stored = lax.dynamic_update_index_in_dim(stored, logits, block, 0)]
    pallas_call x0 -> x1, Pallas kernels: none -> 55.2 us  [attend(): pl.pallas_call(attend_kernel, out_shape=jax.ShapeDtypeStruct((ROWS, GROUP...]
    dynamic_slice x16 -> x0, local copies, waits for them, and re-layouts: 17.3 us -> none  [the longest x8 8.66 us: logits_of(): lax.dynamic_slice_in_dim(keys_pad, key_start, KB + CK - 1, 0)]
    dot_general x24 -> x0, matrix products: 16.6 us -> none  [the longest x8 7.13 us: second_active(): jnp.einsum('gab,gbrk->gark', mix_groups, grouped)]
    another operation x9 -> x1, other arithmetic: 16.9 us -> 0.74 us
    reduce_max x8 -> x0, other arithmetic: 15.6 us -> none  [first_active(): new_peak = jnp.maximum(row_peak, jnp.max(logits, axis=-1))]
    broadcast_in_dim x4 -> x0, local copies, waits for them, and re-layouts: 7.94 us -> none  [the longest x1 7.9 us: attend(): jnp.zeros((block_count, head_count, row_count, KB), jnp.float32)]
    all_gather x2, waiting for transfers between devices: 58.6 us -> 66.2 us  [the longest x1 38.8 us: per_device(): values_all = lax.all_gather(value, 'ctx', axis=0, tiled=True)]
  transfers between devices with their start and end apart: 9 -> 9, of which waited for: 8 -> 8; matrix products, arithmetic and copies ran while one was open for 55% -> 4% of each run, Pallas kernels for 0% -> 14%
where the time goes in v1:
time: 401 us; the launch traced here: 399 us
  waiting for transfers between devices  306 us (76%)
  Pallas kernels  55.2 us (14%)
  matrix products  17.1 us (4%)
  between operations  13.6 us (3%)
    reduce_scatter x1, waiting for transfers between devices, per_device(): lax.psum_scatter(partial_out.astype(jnp.bfloat16), 'head', scatter_dimens...  76.3 us
    pallas_call x1, Pallas kernels, attend(): pl.pallas_call(attend_kernel, out_shape=jax.ShapeDtypeStruct((ROWS, GROUP...  55.2 us
    all_gather x1, waiting for transfers between devices, per_device(): features = lax.all_gather(activations, 'head', axis=1, tiled=True)  53.3 us
    all_gather x1, waiting for transfers between devices, per_device(): values_all = lax.all_gather(value, 'ctx', axis=0, tiled=True)  38.8 us
    all_gather x1, waiting for transfers between devices, per_device(): lax.all_gather(w_query, 'ctx', axis=0, tiled=True)  35.9 us
    all_gather x1, waiting for transfers between devices, per_device(): lax.all_gather(w_key, 'ctx', axis=0, tiled=True)  34.7 us
    all_gather x1, waiting for transfers between devices, per_device(): lax.all_gather(w_value, 'ctx', axis=0, tiled=True)  32.9 us
    all_gather x1, waiting for transfers between devices, per_device(): keys_all = lax.all_gather(key, 'ctx', axis=0, tiled=True)  27.4 us
  transfers between devices with their start and end apart: 9, of which 8 were waited for; matrix products, arithmetic and copies ran while one was open for 4% of the time, Pallas kernels for 14%

profile of v1, /device:TPU:98, one launch (start us, length us, event | category | flops | bytes accessed | tf_op | source)
XLA Modules:
  0.0 398.6 jit_solution(4926626102298670201)
XLA Ops:
  6.5 0.7 all-gather.8.cloned.1.call-update
  7.3 0.0 all-gather.10.cloned.1.call-start
  7.3 0.7 all-gather.10.cloned.1.call-update
  8.1 0.7 all-gather.12.cloned.1.call-update
  8.8 0.5 all-gather.16.cloned.1.call-update
  9.3 0.0 all-gather.14.cloned.1.call-start
  9.4 0.7 convert_multiply_fusion
  10.1 0.5 multiply_cosine_fusion
  10.6 53.3 %all-gather.8.cloned.1.call-done = bf16[256,4096]{1,0:T(8,128)(2,1)} async-done(((bf16[256,512]{1,0:T(8,128)(2,1)}), bf16[256,4096]{1,0:T(8,128)(2,1)}) %all-gather.8.cloned.1.call-update) | async-done | bytes 2097168 | tf_op jit(solution)/shard_map/all_gather | solution.py:261
  63.9 35.9 %all-gather.10.cloned.1.call-done = bf16[4096,512]{1,0:T(8,128)(2,1)} async-done(((bf16[256,512]{1,0:T(8,128)(2,1)}), bf16[4096,512]{1,0:T(8,128)(2,1)}) %all-gather.10.cloned.1.call-update) | async-done | bytes 4194320 | tf_op jit(solution)/shard_map/all_gather | solution.py:266
  99.9 4.1 %fusion.2 = f32[256,512]{1,0:T(8,128)S(1)} fusion(bf16[256,4096]{1,0:T(8,128)(2,1)} %all-gather.8.cloned.1.call-done, bf16[4096,512]{1,0:T(8,128)(2,1)} %all-gather.10.cloned.1.call-done), kind=kOutput, calls=%fused_computation.20 | convolution fusion | flops 1073741824 | bytes 6815744 | tf_op jit(solution)/shard_map/dot_general | solution.py:46
  103.9 0.2 reshape.79
  104.1 34.7 %all-gather.12.cloned.1.call-done = bf16[4096,512]{1,0:T(8,128)(2,1)} async-done(((bf16[256,512]{1,0:T(8,128)(2,1)}), bf16[4096,512]{1,0:T(8,128)(2,1)}) %all-gather.12.cloned.1.call-update) | async-done | bytes 4194320 | tf_op jit(solution)/shard_map/all_gather | solution.py:262
  138.8 3.4 fusion.3
  142.3 0.2 reshape.80
  142.5 0.7 subtract_convert_fusion
  143.2 0.7 pad_maximum_fusion.1
  143.9 0.7 copy.16
  144.7 0.0 all-gather.18.cloned.1.call-start
  144.7 32.9 %all-gather.16.cloned.1.call-done = bf16[4096,512]{1,0:T(8,128)(2,1)} async-done(((bf16[256,512]{1,0:T(8,128)(2,1)}), bf16[4096,512]{1,0:T(8,128)(2,1)}) %all-gather.16.cloned.1.call-update) | async-done | bytes 4194320 | tf_op jit(solution)/shard_map/all_gather | solution.py:264
  177.7 4.8 %convolution_convert_fusion.1 = bf16[256,512]{1,0:T(8,128)(2,1)} fusion(bf16[256,4096]{1,0:T(8,128)(2,1)} %all-gather.8.cloned.1.call-done, bf16[4096,512]{1,0:T(8,128)(2,1)} %all-gather.16.cloned.1.call-done), kind=kOutput, calls=%fused_computation.1 | convolution fusion | flops 1073872896 | bytes 6553600 | tf_op jit(solution)/shard_map/dot_general | solution.py:46
  182.5 0.0 all-gather.20.cloned.1.call-start
  182.5 0.7 all-gather.20.cloned.1.call-update
  183.2 0.1 fusion.1
  183.3 2.1 collective-permute-start
  185.5 2.8 collective-permute-done
  188.3 0.7 pad_maximum_fusion.q_ref
  189.0 27.4 %all-gather.14.cloned.1.call-done.k_ref = bf16[4096,512]{1,0:T(8,128)(2,1)} async-done(((bf16[256,512]{1,0:T(8,128)(2,1)}), bf16[4096,512]{1,0:T(8,128)(2,1)}) %all-gather.14.cloned.1.call-update) | async-done | bytes 4194320 | tf_op jit(solution)/shard_map/all_gather | solution.py:268
  216.5 38.8 %all-gather.18.cloned.1.call-done.v_ref = bf16[4096,512]{1,0:T(8,128)(2,1)} async-done(((bf16[256,512]{1,0:T(8,128)(2,1)}), bf16[4096,512]{1,0:T(8,128)(2,1)}) %all-gather.18.cloned.1.call-update) | async-done | bytes 4194320 | tf_op jit(solution)/shard_map/all_gather | solution.py:269
  255.3 55.2 %attend.1 = bf16[256,512]{1,0:T(8,128)(2,1)} custom-call(s32[1]{0:T(128)} %bitcast.place_ref, f32[4,66]{1,0:T(4,128)} %kern_ref.1, f32[4,4]{1,0:T(4,128)} %mix_ref.1, bf16[264,512]{1,0:T(8,128)(2,1)} %pad_maximum_fusion.q_ref, bf16[4096,512]{1,0:T(8,128)(2,1)} %all-gather.14.cloned.1.call-done.k_ref, bf16[4096,512]{1,0:T(8,128)(2,1)} %all-gather.18.cloned.1.call-done.v_ref, ...), custom_call_target="tpu_custom_call" | custom-call | tf_op jit(solution)/shard_map/attend/pallas_call | solution.py:236
  310.5 4.9 %convolution_convert_fusion = bf16[256,4096]{1,0:T(8,128)(2,1)} fusion(bf16[256,512]{1,0:T(8,128)(2,1)} %attend.1, bf16[512,4096]{1,0:T(8,128)(2,1)} %all-gather.20.cloned.1.call-done), kind=kOutput, calls=%fused_computation | convolution fusion | flops 1074790400 | bytes 6553600 | tf_op jit(solution)/shard_map/dot_general | solution.py:281
  315.4 76.3 %reduce-scatter.2.cloned.1.call-done = bf16[256,512]{1,0:T(8,128)(2,1)} async-done(((bf16[256,4096]{1,0:T(8,128)(2,1)}), bf16[256,512]{1,0:T(8,128)(2,1)}) %reduce-scatter.2.cloned.1.call-update) | async-done | bytes 262160 | tf_op jit(solution)/shard_map/reduce_scatter | solution.py:284
  (13 shorter events, 0.2 us)
Async XLA Ops:
  6.5 57.4 %all-gather.8.cloned.1.call-start = ((), (), s32[]{:S(2)}) async-start(), calls=%async_computation.1 | async-start | bytes 2359296 | tf_op jit(solution)/shard_map/all_gather | solution.py:261
  7.3 92.6 %all-gather.10.cloned.1.call-start = ((), (), s32[]{:S(2)}) async-start(), calls=%async_computation.2 | async-start | bytes 4456448 | tf_op jit(solution)/shard_map/all_gather | solution.py:266
  8.0 130.8 %all-gather.12.cloned.1.call-start = ((), (), s32[]{:S(2)}) async-start(), calls=%async_computation.3 | async-start | bytes 4456448 | tf_op jit(solution)/shard_map/all_gather | solution.py:262
  8.7 168.9 %all-gather.16.cloned.1.call-start = ((), (), s32[]{:S(2)}) async-start(), calls=%async_computation.5 | async-start | bytes 4456448 | tf_op jit(solution)/shard_map/all_gather | solution.py:264
  9.3 207.2 %all-gather.14.cloned.1.call-start = ((), (), s32[]{:S(2)}) async-start(), calls=%async_computation.4 | async-start | bytes 4456448 | tf_op jit(solution)/shard_map/all_gather | solution.py:268
  63.9 74.9 %copy-start = (bf16[256,4096]{1,0:T(8,128)(2,1)S(1)}, bf16[256,4096]{1,0:T(8,128)(2,1)}, u32[]{:S(2)}) copy-start(bf16[256,4096]{1,0:T(8,128)(2,1)} %all-gather.8.cloned.1.call-done) | copy-start | bytes 6291460
  144.7 110.6 %all-gather.18.cloned.1.call-start = ((), (), s32[]{:S(2)}) async-start(), calls=%async_computation.6 | async-start | bytes 4456448 | tf_op jit(solution)/shard_map/all_gather | solution.py:269
  182.5 128.1 %all-gather.20.cloned.1.call-start = ((), (), s32[]{:S(2)}) async-start(), calls=%async_computation.7 | async-start | bytes 4456448 | tf_op jit(solution)/shard_map/all_gather | solution.py:282
  183.2 208.5 %reduce-scatter.2.cloned.1.call-start = ((), (), s32[]{:S(2)}) async-start(), calls=%async_computation.8 | async-start | bytes 2359296 | tf_op jit(solution)/shard_map/reduce_scatter | solution.py:284
  183.3 5.0 %collective-permute-start = (bf16[8,512]{1,0:T(8,128)(2,1)S(1)}, bf16[8,512]{1,0:T(8,128)(2,1)S(1)}, u32[]{:S(2)}, u32[]{:S(2)}) collective-permute-start(bf16[8,512]{1,0:T(8,128)(2,1)S(1)} %bitcast.27), channel_id=1, source_target_pairs={{0,8},{8,16},{16,24},{24,32},{32,40},{40,48},{48,56},{56,64},{64,7... | collective-permute-start | bytes 24584 | tf_op jit(solution)/shard_map/ppermute | solution.py:24
Sparse Core Ops, SparseCore 0:
  9.5 54.3 all-gather.7
  65.6 34.1 all-gather.9
  101.6 37.2 all-gather.11
  140.4 37.2 all-gather.15
  179.2 37.2 all-gather.13
  218.0 37.2 all-gather.17
  256.9 45.5 all-gather.19
  315.5 76.1 reduce-scatter.1

commit v2 on v1

--- a/solution.py
+++ b/solution.py
@@ -18,32 +18,390 @@
 BAND = 10
 
 
-def passed_along(value, axis, steps):
-    count = lax.axis_size(axis)
-    leading, last = (max(0, -steps), min(count, count - steps))
-    return lax.ppermute(value, axis, [(source, source + steps) for source in range(leading, last)])
-
-
-def rope(projected, positions):
-    row_count = projected.shape[0]
-    head_count = projected.shape[1] // HD
-    shaped = projected.reshape(row_count, head_count, HD)
-    half_size = HD // 2
-    exponents = jnp.arange(half_size, dtype=jnp.float32) * (2.0 / HD)
-    inverse = jnp.exp(-exponents * math.log(500000.0))
-    angle = (positions.astype(jnp.float32) * 0.25)[:, None, None] * inverse[None, None, :]
-    cosine = jnp.cos(angle)
-    sine = jnp.sin(angle)
-    lower_half = shaped[..., :half_size]
-    upper_half = shaped[..., half_size:]
-    rotated_rows = jnp.concatenate(
-        [lower_half * cosine - upper_half * sine, upper_half * cosine + lower_half * sine], -1
+MESH = pl.DeviceIdType.MESH
+
+
+class Places:
+    def __init__(self):
+        self.ctx = lax.axis_index("ctx")
+        self.head = lax.axis_index("head")
+        self.col = lax.div(self.ctx, 8)
+        self.z = lax.rem(lax.div(self.ctx, 2), 4)
+        self.core = lax.rem(self.ctx, 2)
+        self.y = lax.rem(self.head, 4)
+        self.far = lax.div(self.head, 4)
+
+    def ctx_at(self, flip_col=False, dz=0, flip_core=False):
+        col = 1 - self.col if flip_col else self.col
+        core = 1 - self.core if flip_core else self.core
+        return col * 8 + lax.rem(self.z + dz + 4, 4) * 2 + core
+
+    def head_at(self, flip=False, dy=0):
+        far = 1 - self.far if flip else self.far
+        return far * 4 + lax.rem(self.y + dy + 4, 4)
+
+
+def greet(targets):
+    barrier = pltpu.get_barrier_semaphore()
+    for target in targets:
+        pl.semaphore_signal(barrier, inc=1, device_id=target, device_id_type=MESH)
+    pl.semaphore_wait(barrier, len(targets))
+
+
+class Gather:
+    def __init__(self, at, own, buf, rows, send, recv):
+        self.at, self.own, self.buf, self.rows, self.send, self.recv = at, own, buf, rows, send, recv
+        self.sib = {"ctx": at.ctx_at(flip_core=True)}
+        self.xn = {"ctx": at.ctx_at(flip_col=True)}
+        self.up = {"ctx": at.ctx_at(dz=1)}
+        self.down = {"ctx": at.ctx_at(dz=-1)}
+        self.sent = []
+
+    def slot(self, index, half=None):
+        size = self.rows if half is None else self.rows // 2
+        first = index * self.rows + (size if half == 1 else 0)
+        return self.buf.at[pl.ds(pl.multiple_of(first, size), size), :]
+
+    def put(self, event, target, src, dst):
+        copy = pltpu.make_async_remote_copy(
+            src_ref=src, dst_ref=dst, send_sem=self.send.at[event], recv_sem=self.recv.at[event],
+            device_id=target, device_id_type=MESH,
+        )
+        copy.start()
+        self.sent.append(copy)
+
+    def pass_on(self, event, target, index, half=None):
+        piece = self.slot(index, half)
+        self.put(event, target, piece, piece)
+
+    def arrive(self, event, index, half=None):
+        piece = self.slot(index, half)
+        pltpu.make_async_remote_copy(
+            src_ref=piece, dst_ref=piece, send_sem=self.send.at[event],
+            recv_sem=self.recv.at[event], device_id=self.sib, device_id_type=MESH,
+        ).wait_recv()
+
+    def first(self):
+        dst = self.slot(self.at.ctx)
+        self.put(2, self.up, self.own, dst)
+        self.put(3, self.down, self.own, dst)
+        self.put(1, self.xn, self.own, dst)
+        self.put(0, self.sib, self.own, dst)
+
+    def second(self):
+        at = self.at
+        index = at.ctx_at(flip_col=True)
+        self.arrive(1, index)
+        self.pass_on(4, self.up, index)
+        self.pass_on(5, self.down, index)
+        self.pass_on(9, self.sib, index)
+        index = at.ctx_at(dz=-1)
+        self.arrive(2, index)
+        self.pass_on(6, self.up, index, 0)
+        self.pass_on(10, self.sib, index)
+        index = at.ctx_at(dz=1)
+        self.arrive(3, index)
+        self.pass_on(7, self.down, index, 1)
+        self.pass_on(11, self.sib, index)
+
+    def third(self):
+        at = self.at
+        index = at.ctx_at(dz=2)
+        self.arrive(6, index, 0)
+        self.arrive(7, index, 1)
+        self.pass_on(8, self.xn, index)
+        self.pass_on(14, self.sib, index)
+        for event, dz, on in ((4, -1, 12), (5, 1, 13)):
+            index = at.ctx_at(flip_col=True, dz=dz)
+            self.arrive(event, index)
+            self.pass_on(on, self.sib, index)
+
+    def last(self):
+        at = self.at
+        index = at.ctx_at(flip_col=True, dz=2)
+        self.arrive(8, index)
+        self.pass_on(15, self.sib, index)
+
+    def whole(self):
+        at = self.at
+        for event, flip_col, dz in (
+            (0, False, 0), (9, True, 0), (10, False, -1), (11, False, 1),
+            (12, True, -1), (13, True, 1), (14, False, 2), (15, True, 2),
+        ):
+            self.arrive(event, at.ctx_at(flip_col=flip_col, dz=dz, flip_core=True))
+
+    def close(self):
+        for copy in self.sent:
+            copy.wait_send()
+
+
+class Features:
+    def __init__(self, at, own, buf, send, recv):
+        self.at, self.own, self.buf, self.send, self.recv = at, own, buf, send, recv
+        self.partner = {"head": at.head_at(flip=True)}
+        self.up = {"head": at.head_at(dy=1)}
+        self.down = {"head": at.head_at(dy=-1)}
+        self.sent = []
+
+    def slot(self, index, half=None):
+        cols = pl.ds(pl.multiple_of(index * 512, 512), 512)
+        if half is None:
+            return self.buf.at[:, cols]
+        return self.buf.at[pl.ds(half * (ROWS // 2), ROWS // 2), cols]
+
+    put, pass_on = Gather.put, Gather.pass_on
+
+    def arrive(self, event, index, half=None):
+        piece = self.slot(index, half)
+        pltpu.make_async_remote_copy(
+            src_ref=piece, dst_ref=piece, send_sem=self.send.at[event],
+            recv_sem=self.recv.at[event], device_id=self.partner, device_id_type=MESH,
+        ).wait_recv()
+
+    def first(self):
+        dst = self.slot(self.at.head)
+        self.put(0, self.partner, self.own, dst)
+        self.put(1, self.up, self.own, dst)
+        self.put(2, self.down, self.own, dst)
+
+    def second(self):
+        at = self.at
+        index = at.head_at(flip=True)
+        self.arrive(0, index)
+        self.pass_on(3, self.up, index)
+        self.pass_on(4, self.down, index)
+        index = at.head_at(dy=-1)
+        self.arrive(1, index)
+        self.pass_on(5, self.up, index, 0)
+        index = at.head_at(dy=1)
+        self.arrive(2, index)
+        self.pass_on(6, self.down, index, 1)
+
+    def third(self):
+        at = self.at
+        index = at.head_at(flip=True, dy=-1)
+        self.arrive(3, index)
+        self.pass_on(7, self.up, index, 0)
+        index = at.head_at(flip=True, dy=1)
+        self.arrive(4, index)
+        self.pass_on(8, self.down, index, 1)
+
+    def whole(self):
+        at = self.at
+        for event, flip in ((5, False), (7, True)):
+            index = at.head_at(flip=flip, dy=2)
+            self.arrive(event, index, 0)
+            self.arrive(event + 1, index, 1)
+
+    close = Gather.close
+
+
+def project_kernel(
+    x_ref, wk_ref, wv_ref, wq_ref, wo_ref, cos_ref, sin_ref,
+    q_out, rim_out, k_out, v_out, wo_out,
+    x_buf, w_bufs, made, send, recv, x_send, x_recv, here, rim_sems,
+):
+    at = Places()
+    after = {"ctx": lax.rem(at.ctx + 1, 16)}
+    greet(
+        [{"ctx": at.ctx_at(flip_core=True)}, {"ctx": at.ctx_at(flip_col=True)}]
+        + [{"ctx": at.ctx_at(dz=1)}, {"ctx": at.ctx_at(dz=-1)}]
+        + [{"head": at.head_at(dy=1)}, {"head": at.head_at(dy=-1)}, {"head": at.head_at(flip=True)}]
+        + [after, {"ctx": lax.rem(at.ctx + 15, 16)}]
     )
-    return rotated_rows.reshape(row_count, head_count * HD)
-
-
-def add_rows(left, piece):
-    return jnp.dot(left, piece, preferred_element_type=jnp.float32)
+
+    def gather(t, own, buf, rows):
+        return Gather(at, own, buf, rows, send.at[t], recv.at[t])
+
+    feats = Features(at, x_ref, x_buf, x_send, x_recv)
+    wk = gather(0, wk_ref, w_bufs.at[0], ROWS)
+    wv = gather(1, wv_ref, w_bufs.at[1], ROWS)
+    wq = gather(2, wq_ref, w_bufs.at[2], ROWS)
+    own_slot = pl.ds(pl.multiple_of(at.ctx * ROWS, ROWS), ROWS)
+    keys = gather(3, k_out.at[own_slot], k_out, ROWS)
+    values = gather(4, v_out.at[own_slot], v_out, ROWS)
+    wo = gather(5, wo_ref, wo_out, 2 * ROWS)
+
+    wk.first()
+    feats.first()
+    own = [
+        pltpu.make_async_copy(x_ref, feats.slot(at.head), here.at[0]),
+        pltpu.make_async_copy(wk_ref, wk.slot(at.ctx), here.at[1]),
+        pltpu.make_async_copy(wv_ref, wv.slot(at.ctx), here.at[2]),
+        pltpu.make_async_copy(wq_ref, wq.slot(at.ctx), here.at[3]),
+        pltpu.make_async_copy(wo_ref, wo.slot(at.ctx), here.at[4]),
+    ]
+    for copy in own:
+        copy.start()
+
+    def project(t):
+        return jnp.dot(x_buf[...], w_bufs[t], preferred_element_type=jnp.float32)
+
+    def rotate(projected):
+        turned = []
+        for h in range(GROUP):
+            part = projected[:, h * HD : (h + 1) * HD]
+            turned.append(part * cos_ref[...] + pltpu.roll(part, HD // 2, 1) * sin_ref[...])
+        return jnp.concatenate(turned, 1)
+
+    def keep(index, value, dst):
+        made[index] = value.astype(jnp.bfloat16)
+        copy = pltpu.make_async_copy(made.at[index], dst, here.at[5 + index])
+        copy.start()
+        copy.wait()
+
+    wk.second()
+    feats.second()
+    wv.first()
+    wk.third()
+    feats.third()
+    wv.second()
+    wq.first()
+    wk.last()
+    for copy in own:
+        copy.wait()
+    feats.whole()
+    wk.whole()
+    keep(0, rotate(project(0)), k_out.at[own_slot])
+    wv.third()
+    wq.second()
+    keys.first()
+    wv.last()
+    wv.whole()
+    keep(1, project(1), v_out.at[own_slot])
+    wq.third()
+    keys.second()
+    values.first()
+    wq.last()
+    wq.whole()
+    keep(2, rotate(project(2)), q_out)
+    rim = pltpu.make_async_remote_copy(
+        src_ref=q_out.at[pl.ds(ROWS - 16, 16)], dst_ref=rim_out,
+        send_sem=rim_sems.at[0], recv_sem=rim_sems.at[1], device_id=after, device_id_type=MESH,
+    )
+    rim.start()
+    keys.third()
+    values.second()
+    wo.first()
+    keys.last()
+    values.third()
+    wo.second()
+    values.last()
+    wo.third()
+    wo.last()
+    keys.whole()
+    values.whole()
+    wo.whole()
+    rim.wait()
+    for each in (feats, wk, wv, wq, keys, values, wo):
+        each.close()
+
+
+def project(x, wk, wv, wq, wo, cosine, sine):
+    any_ref = pl.BlockSpec(memory_space=pl.ANY)
+    vmem = pl.BlockSpec(memory_space=pltpu.VMEM)
+    width = GROUP * HD
+    shape = lambda *dims: jax.ShapeDtypeStruct(dims, jnp.bfloat16)
+    return pl.pallas_call(
+        project_kernel,
+        out_shape=(
+            shape(ROWS, width), shape(16, width), shape(TOKENS, width), shape(TOKENS, width),
+            shape(16 * width, ROWS),
+        ),
+        in_specs=[any_ref] * 5 + [vmem] * 2,
+        out_specs=(any_ref,) * 5,
+        scratch_shapes=[
+            pltpu.VMEM((ROWS, TOKENS), jnp.bfloat16),
+            pltpu.VMEM((3, TOKENS, width), jnp.bfloat16),
+            pltpu.VMEM((3, ROWS, width), jnp.bfloat16),
+            pltpu.SemaphoreType.DMA((6, 16)),
+            pltpu.SemaphoreType.DMA((6, 16)),
+            pltpu.SemaphoreType.DMA((9,)),
+            pltpu.SemaphoreType.DMA((9,)),
+            pltpu.SemaphoreType.DMA((8,)),
+            pltpu.SemaphoreType.DMA((2,)),
+        ],
+        compiler_params=pltpu.CompilerParams(
+            collective_id=1, has_side_effects=True, vmem_limit_bytes=40 * 1024 * 1024
+        ),
+        name="project",
+    )(x, wk, wv, wq, wo, cosine, sine)
+
+
+def reduce_kernel(p_ref, o_ref, up_half, down_half, up_full, down_full, up_sum, down_sum, give, got, send, recv):
+    at = Places()
+    up = {"head": at.head_at(dy=1)}
+    down = {"head": at.head_at(dy=-1)}
+    partner = {"head": at.head_at(flip=True)}
+    greet([up, down, partner])
+    half = ROWS // 2
+    top, low = pl.ds(0, half), pl.ds(half, half)
+    y_up = lax.rem(at.y + 1, 4)
+    y_down = lax.rem(at.y + 3, 4)
+    y_far = lax.rem(at.y + 2, 4)
+
+    def copy(event, target, src, dst):
+        made = pltpu.make_async_remote_copy(
+            src_ref=src, dst_ref=dst, send_sem=send.at[event], recv_sem=recv.at[event],
+            device_id=target, device_id_type=MESH,
+        )
+        made.start()
+        return made
+
+    c0 = copy(0, up, p_ref.at[y_far, :, top], up_half)
+    c1 = copy(1, down, p_ref.at[y_far, :, low], down_half)
+
+    def add(left, right):
+        return (left.astype(jnp.float32) + right.astype(jnp.float32)).astype(jnp.bfloat16)
+
+    up_sum[:, low] = p_ref[y_up, :, low]
+    down_sum[:, top] = p_ref[y_down, :, top]
+    c0.wait_recv()
+    up_sum[:, top] = add(p_ref[y_up, :, top], up_half[...])
+    c2 = copy(2, up, up_sum, up_full)
+    c1.wait_recv()
+    down_sum[:, low] = add(p_ref[y_down, :, low], down_half[...])
+    c3 = copy(3, down, down_sum, down_full)
+    c2.wait_recv()
+    c3.wait_recv()
+
+    def total(far):
+        return (
+            p_ref[at.y, far].astype(jnp.float32)
+            + up_full[far].astype(jnp.float32)
+            + down_full[far].astype(jnp.float32)
+        )
+
+    give[...] = total(1 - at.far).astype(jnp.bfloat16)
+    c4 = copy(4, partner, give, got)
+    mine = total(at.far)
+    c4.wait_recv()
+    o_ref[...] = (mine + got[...].astype(jnp.float32)).astype(jnp.bfloat16)
+    for made in (c0, c1, c2, c3, c4):
+        made.wait_send()
+
+
+def reduce_over_head(partial):
+    vmem = pl.BlockSpec(memory_space=pltpu.VMEM)
+    width = GROUP * HD
+    buf = lambda *dims: pltpu.VMEM(dims, jnp.bfloat16)
+    return pl.pallas_call(
+        reduce_kernel,
+        out_shape=jax.ShapeDtypeStruct((ROWS, width), jnp.bfloat16),
+        in_specs=[vmem],
+        out_specs=vmem,
+        scratch_shapes=[
+            buf(2, ROWS // 2, width), buf(2, ROWS // 2, width),
+            buf(2, ROWS, width), buf(2, ROWS, width), buf(2, ROWS, width), buf(2, ROWS, width),
+            buf(ROWS, width), buf(ROWS, width),
+            pltpu.SemaphoreType.DMA((5,)),
+            pltpu.SemaphoreType.DMA((5,)),
+        ],
+        compiler_params=pltpu.CompilerParams(
+            collective_id=2, has_side_effects=True, vmem_limit_bytes=32 * 1024 * 1024
+        ),
+        name="reduce_over_head",
+    )(partial)
 
 
 def dot_nt(left, right):
@@ -53,8 +411,8 @@
 
 
 def attend_kernel(
-    place_ref, kern_ref, mix_ref, q_ref, k_ref, v_ref, gain_ref, o_ref,
-    q32, k32, qt, kc, lg, band, acc, tail,
+    place_ref, kern_ref, mix_ref, q_ref, rim_ref, k_ref, v_ref, wo_ref, gain_ref, o_ref,
+    normed, q32, k32, qt, kc, lg, band, acc, tail,
 ):
     place = place_ref[0]
     r0 = place * ROWS
@@ -66,7 +424,9 @@
 
     for h in range(GROUP):
         cols = slice(h * HD, (h + 1) * HD)
-        q32[h] = q_ref[:, cols].astype(jnp.float32)
+        q32[h, 8:] = q_ref[:, cols].astype(jnp.float32)
+        rim = rim_ref[:, cols].astype(jnp.float32)[8:]
+        q32[h, :8] = jnp.where(place > 0, rim, 0.0)
         k32[h, :FRONT] = jnp.zeros((FRONT, HD), jnp.float32)
         k32[h, pl.ds(pl.multiple_of(FRONT + blocks * KB, 8), 8)] = jnp.zeros((8, HD), jnp.float32)
 
@@ -227,18 +587,30 @@
         for g in range(1, GROUP):
             total = total + mix_ref[h, g] * (acc[g, :, cols] * tail[g])
         rms = jnp.sqrt(jnp.mean(total * total, axis=1, keepdims=True) + 1e-05)
-        o_ref[:, cols] = (total / rms * gain_ref[:, cols]).astype(jnp.bfloat16)
-
-
-def attend(place, query_ext, keys, values, kernel, mixing, gain):
+        normed[:, cols] = (total / rms * gain_ref[:, cols]).astype(jnp.bfloat16)
+
+    width = GROUP * HD
+
+    def out_block(b, _):
+        rows = pl.ds(pl.multiple_of(b * width, width), width)
+        piece = jnp.dot(normed[...], wo_ref[rows], preferred_element_type=jnp.float32)
+        far, y, part = lax.div(b, 8), lax.rem(lax.div(b, 2), 4), lax.rem(b, 2)
+        o_ref[y, far, :, pl.ds(pl.multiple_of(part * ROWS, ROWS), ROWS)] = piece.astype(jnp.bfloat16)
+        return 0
+
+    lax.fori_loop(0, 16, out_block, 0)
+
+
+def attend(place, query, rim, keys, values, wo, kernel, mixing, gain):
     smem = pl.BlockSpec(memory_space=pltpu.SMEM)
     vmem = pl.BlockSpec(memory_space=pltpu.VMEM)
     return pl.pallas_call(
         attend_kernel,
-        out_shape=jax.ShapeDtypeStruct((ROWS, GROUP * HD), jnp.bfloat16),
-        in_specs=[smem, smem, smem, vmem, vmem, vmem, vmem],
+        out_shape=jax.ShapeDtypeStruct((4, 2, ROWS, GROUP * HD), jnp.bfloat16),
+        in_specs=[smem, smem, smem, vmem, vmem, vmem, vmem, vmem, vmem],
         out_specs=vmem,
         scratch_shapes=[
+            pltpu.VMEM((ROWS, GROUP * HD), jnp.bfloat16),
             pltpu.VMEM((GROUP, ROWS + 8, HD), jnp.float32),
             pltpu.VMEM((GROUP, FRONT + TOKENS + 16, HD), jnp.float32),
             pltpu.VMEM((GROUP, ROWS, CK * HD), jnp.bfloat16),
@@ -250,40 +622,26 @@
         ],
         compiler_params=pltpu.CompilerParams(vmem_limit_bytes=62 * 1024 * 1024),
         name="attend",
-    )(place, kernel, mixing, query_ext, keys, values, gain)
+    )(place, kernel, mixing, query, rim, keys, values, wo, gain)
 
 
 def per_device(
     activations, positions, w_query, w_key, w_value, conv_kernel, head_mix, out_gain, w_out
 ):
-    row_count = activations.shape[0]
-    ctx_place = lax.axis_index("ctx")
-    features = lax.all_gather(activations, "head", axis=1, tiled=True)
-    key_proj = add_rows(features, lax.all_gather(w_key, "ctx", axis=0, tiled=True))
-    key = rope(key_proj, positions).astype(jnp.bfloat16)
-    value_proj = add_rows(features, lax.all_gather(w_value, "ctx", axis=0, tiled=True))
-    value = value_proj.astype(jnp.bfloat16)
-    query_proj = add_rows(features, lax.all_gather(w_query, "ctx", axis=0, tiled=True))
-    query = rope(query_proj, positions).astype(jnp.bfloat16)
-    keys_all = lax.all_gather(key, "ctx", axis=0, tiled=True)
-    values_all = lax.all_gather(value, "ctx", axis=0, tiled=True)
-    rim_rows = passed_along(query[row_count - 8 :], "ctx", 1)
-    query_ext = jnp.concatenate([rim_rows, query], 0)
-    normed = attend(
-        ctx_place.astype(jnp.int32).reshape(1),
-        query_ext,
-        keys_all,
-        values_all,
-        conv_kernel,
-        head_mix,
-        out_gain.reshape(1, -1),
+    exponents = jnp.arange(HD // 2, dtype=jnp.float32) * (2.0 / HD)
+    inverse = jnp.exp(-exponents * math.log(500000.0))
+    angle = (positions.astype(jnp.float32) * 0.25)[:, None] * inverse[None, :]
+    cosine = jnp.cos(angle)
+    sine = jnp.sin(angle)
+    query, rim, keys, values, wo = project(
+        activations, w_key, w_value, w_query, w_out,
+        jnp.concatenate([cosine, cosine], 1), jnp.concatenate([-sine, sine], 1),
     )
-    partial_out = jnp.dot(
-        normed, lax.all_gather(w_out, "ctx", axis=1, tiled=True), preferred_element_type=jnp.float32
+    partial = attend(
+        lax.axis_index("ctx").astype(jnp.int32).reshape(1),
+        query, rim, keys, values, wo, conv_kernel, head_mix, out_gain.reshape(1, -1),
     )
-    return lax.psum_scatter(
-        partial_out.astype(jnp.bfloat16), "head", scatter_dimension=1, tiled=True
-    )
+    return reduce_over_head(partial)
 
 
 def solution(mesh):

time: 401 us -> 206 us (0.51)
  waiting for transfers between devices: 306 us -> 0 us
  Pallas kernels: 55.2 us -> 190 us
  matrix products: 17.1 us -> 0 us
  between operations: 13.6 us -> 0.06 us
  local copies, waits for them, and re-layouts: 1.15 us -> 14.2 us
    all_gather x7 -> x0, waiting for transfers between devices: 223 us -> none  [the longest x1 53.3 us: per_device(): features = lax.all_gather(activations, 'head', axis=1, tiled=True)]
    pallas_call x1 -> x3, Pallas kernels: 55.2 us -> 190 us  [the longest x1 98.9 us: project(): pl.pallas_call(project_kernel, out_shape=(shape(ROWS, width), shape(16, w...]
    reduce_scatter x1 -> x0, waiting for transfers between devices: 76.3 us -> none  [per_device(): lax.psum_scatter(partial_out.astype(jnp.bfloat16), 'head', scatter_dimens...]
    dot_general x4 -> x0, matrix products: 17.1 us -> none  [the longest x3 12.3 us: add_rows(): return jnp.dot(left, piece, preferred_element_type=jnp.float32)]
    unnamed x5 -> x23, local copies, waits for them, and re-layouts: 0.79 us -> 14.2 us
  transfers between devices with their start and end apart: 9 -> 0, of which waited for: 8 -> 0; matrix products, arithmetic and copies ran while one was open for 4% -> 0% of each run, Pallas kernels for 14% -> 0%
where the time goes in v2:
time: 206 us
  Pallas kernels  190 us (92%)
  local copies, waits for them, and re-layouts  14.2 us (7%)
    pallas_call x1, Pallas kernels, project(): pl.pallas_call(project_kernel, out_shape=(shape(ROWS, width), shape(16, w...  98.9 us
    pallas_call x1, Pallas kernels, attend(): pl.pallas_call(attend_kernel, out_shape=jax.ShapeDtypeStruct((4, 2, ROWS,...  60.7 us
    pallas_call x1, Pallas kernels, reduce_over_head(): pl.pallas_call(reduce_kernel, out_shape=jax.ShapeDtypeStruct((ROWS, width...  30.5 us
    unnamed x23, local copies, waits for them, and re-layouts  14.2 us

profile of v2, /device:TPU:98, one launch (start us, length us, event | category | flops | bytes accessed | tf_op | source)
XLA Modules:
  0.0 205.8 jit_solution(8399628454656450062)
XLA Ops:
  0.0 0.7 convert_multiply_fusion
  0.7 0.5 fusion
  1.2 0.1 pad_maximum_fusion
  1.4 0.0 copy-start.5
  1.4 0.9 copy-done.5
  2.3 0.0 copy-start.6
  2.3 0.9 copy-done.6
  3.3 0.0 copy-start.7
  3.3 0.9 copy-done.7
  4.2 0.0 copy-start.8
  4.2 0.9 copy-done.8
  5.2 0.0 copy-start.9
  5.2 0.9 copy-done.9
  6.1 98.9 %project.1 = (bf16[256,512]{1,0:T(8,128)(2,1)S(1)}, bf16[16,512]{1,0:T(8,128)(2,1)S(1)}, bf16[4096,512]{1,0:T(8,128)(2,1)S(1)}, bf16[4096,512]{1,0:T(8,128)(2,1)S(1)}, bf16[8192,256]{1,0:T(8,128)(2,1)S(1)}) custom-call(bf16[256,512]{1,0:T(8,128)(2,1)S(1)} %copy-done.5, bf16[256,512]{1,0:T(8,128)(2,1)S(1)} %copy-done.6, bf16[256,512]{1,0:T(8,128)(2,1)S(1)} %copy-done.7, ...), custom_call_target="tpu_custom_call" | custom-call | tf_op jit(solution)/shard_map/project/pallas_call | solution.py:305
  105.0 0.0 copy-start.1
  105.0 1.9 copy-done.1
  107.0 0.0 copy-start.2
  107.0 2.0 copy-done.2
  108.9 0.0 copy-start.3
  108.9 2.0 copy-done.3
  110.9 0.0 copy-start.4
  110.9 0.7 copy-done.4
  111.6 0.0 copy-start.10
  111.6 0.6 copy-done.10
  112.2 60.7 %attend.1.p_ref = bf16[4,2,256,512]{3,2,1,0:T(8,128)(2,1)} custom-call(s32[1]{0:T(128)} %bitcast.place_ref, f32[4,66]{1,0:T(4,128)} %kern_ref.1, f32[4,4]{1,0:T(4,128)} %mix_ref.1, bf16[256,512]{1,0:T(8,128)(2,1)} %copy-done.4, bf16[16,512]{1,0:T(8,128)(2,1)} %copy-done.10, bf16[4096,512]{1,0:T(8,128)(2,1)} %copy-done.1, bf16[4096,512]{1,0:T(8,128)(2,1)} %copy-done.2, ...), custom_call_target="tpu_custom_call" | custom-call | tf_op jit(solution)/shard_map/attend/pallas_call | solution.py:607
  173.0 0.0 copy-start
  173.0 1.6 copy-done
  174.5 30.5 %reduce_over_head.1 = bf16[256,512]{1,0:T(8,128)(2,1)S(1)} custom-call(bf16[4,2,256,512]{3,2,1,0:T(8,128)(2,1)S(1)} %copy-done), custom_call_target="tpu_custom_call" | custom-call | tf_op jit(solution)/shard_map/reduce_over_head/pallas_call | solution.py:388
  205.1 0.7 copy.11
  (1 shorter events, 0.0 us)
Async XLA Ops:
  1.4 1.0 copy-start.5
  2.3 0.9 copy-start.6
  3.3 0.9 copy-start.7
  4.2 0.9 copy-start.8
  5.2 0.9 copy-start.9
  105.0 1.9 copy-start.1
  107.0 2.0 copy-start.2
  108.9 2.0 copy-start.3
  110.9 0.7 copy-start.4
  111.6 0.6 copy-start.10
  173.0 1.6 copy-start

commit v3 on v2

v3 whole, which is shorter than its diff:
```python
import math

import jax
import jax.numpy as jnp
from jax import lax
from jax.experimental import pallas as pl
from jax.experimental.pallas import tpu as pltpu
from jax.sharding import PartitionSpec as P

HD = 128
GROUP = 4
CQ = 6
CK = 11
KB = 512
ROWS = 256
TOKENS = 4096
HALF = 128
BAND = 10


MESH = pl.DeviceIdType.MESH


class Places:
    def __init__(self):
        self.ctx = lax.axis_index("ctx")
        self.head = lax.axis_index("head")
        self.col = lax.div(self.ctx, 8)
        self.z = lax.rem(lax.div(self.ctx, 2), 4)
        self.core = lax.rem(self.ctx, 2)
        self.y = lax.rem(self.head, 4)
        self.far = lax.div(self.head, 4)

    def ctx_at(self, flip_col=False, dz=0, flip_core=False):
        col = 1 - self.col if flip_col else self.col
        core = 1 - self.core if flip_core else self.core
        return col * 8 + lax.rem(self.z + dz + 4, 4) * 2 + core

    def head_at(self, flip=False, dy=0):
        far = 1 - self.far if flip else self.far
        return far * 4 + lax.rem(self.y + dy + 4, 4)


def greet(targets):
    barrier = pltpu.get_barrier_semaphore()
    for target in targets:
        pl.semaphore_signal(barrier, inc=1, device_id=target, device_id_type=MESH)
    pl.semaphore_wait(barrier, len(targets))


class Gather:
    def __init__(self, at, own, buf, rows, send, recv, base=0):
        self.at, self.own, self.buf, self.rows, self.send, self.recv = at, own, buf, rows, send, recv
        self.base = base
        self.sib = {"ctx": at.ctx_at(flip_core=True)}
        self.xn = {"ctx": at.ctx_at(flip_col=True)}
        self.up = {"ctx": at.ctx_at(dz=1)}
        self.down = {"ctx": at.ctx_at(dz=-1)}

    def slot(self, index, half=None):
        size = self.rows if half is None else self.rows // 2
        first = self.base + index * self.rows + (size if half == 1 else 0)
        return self.buf.at[pl.ds(pl.multiple_of(first, 128), size), :]

    def put(self, event, target, src, dst):
        copy = pltpu.make_async_remote_copy(
            src_ref=src, dst_ref=dst, send_sem=self.send.at[event], recv_sem=self.recv.at[event],
            device_id=target, device_id_type=MESH,
        )
        copy.start()

    def pass_on(self, event, target, index, half=None):
        piece = self.slot(index, half)
        self.put(event, target, piece, piece)

    def arrive(self, event, index, half=None):
        piece = self.slot(index, half)
        pltpu.make_async_remote_copy(
            src_ref=piece, dst_ref=piece, send_sem=self.send.at[event],
            recv_sem=self.recv.at[event], device_id=self.sib, device_id_type=MESH,
        ).wait_recv()

    def first(self):
        dst = self.slot(self.at.ctx)
        self.put(2, self.up, self.own, dst)
        self.put(3, self.down, self.own, dst)
        self.put(1, self.xn, self.own, dst)
        self.put(0, self.sib, self.own, dst)

    def second(self):
        at = self.at
        index = at.ctx_at(flip_col=True)
        self.arrive(1, index)
        self.pass_on(4, self.up, index)
        self.pass_on(5, self.down, index)
        self.pass_on(9, self.sib, index)
        index = at.ctx_at(dz=-1)
        self.arrive(2, index)
        self.pass_on(6, self.up, index, 0)
        self.pass_on(10, self.sib, index)
        index = at.ctx_at(dz=1)
        self.arrive(3, index)
        self.pass_on(7, self.down, index, 1)
        self.pass_on(11, self.sib, index)

    def third(self):
        at = self.at
        index = at.ctx_at(dz=2)
        self.arrive(6, index, 0)
        self.arrive(7, index, 1)
        self.pass_on(8, self.xn, index)
        self.pass_on(14, self.sib, index)
        for event, dz, on in ((4, -1, 12), (5, 1, 13)):
            index = at.ctx_at(flip_col=True, dz=dz)
            self.arrive(event, index)
            self.pass_on(on, self.sib, index)

    def last(self):
        at = self.at
        index = at.ctx_at(flip_col=True, dz=2)
        self.arrive(8, index)
        self.pass_on(15, self.sib, index)

    def whole(self):
        at = self.at
        for event, flip_col, dz in (
            (0, False, 0), (9, True, 0), (10, False, -1), (11, False, 1),
            (12, True, -1), (13, True, 1), (14, False, 2), (15, True, 2),
        ):
            self.arrive(event, at.ctx_at(flip_col=flip_col, dz=dz, flip_core=True))

    halves = (6, 7)
    events = 16

    def close(self):
        for event in range(self.events):
            piece = self.slot(0, 0 if event in self.halves else None)
            pltpu.make_async_remote_copy(
                src_ref=piece, dst_ref=piece, send_sem=self.send.at[event],
                recv_sem=self.recv.at[event], device_id=self.sib, device_id_type=MESH,
            ).wait_send()


class Features:
    def __init__(self, at, own, buf, send, recv):
        self.at, self.own, self.buf, self.send, self.recv = at, own, buf, send, recv
        self.partner = self.sib = {"head": at.head_at(flip=True)}
        self.up = {"head": at.head_at(dy=1)}
        self.down = {"head": at.head_at(dy=-1)}

    def slot(self, index, half=None):
        cols = pl.ds(pl.multiple_of(index * 512, 512), 512)
        if half is None:
            return self.buf.at[:, cols]
        return self.buf.at[pl.ds(half * (ROWS // 2), ROWS // 2), cols]

    put, pass_on = Gather.put, Gather.pass_on

    def arrive(self, event, index, half=None):
        piece = self.slot(index, half)
        pltpu.make_async_remote_copy(
            src_ref=piece, dst_ref=piece, send_sem=self.send.at[event],
            recv_sem=self.recv.at[event], device_id=self.partner, device_id_type=MESH,
        ).wait_recv()

    def first(self):
        dst = self.slot(self.at.head)
        self.put(0, self.partner, self.own, dst)
        self.put(1, self.up, self.own, dst)
        self.put(2, self.down, self.own, dst)

    def second(self):
        at = self.at
        index = at.head_at(flip=True)
        self.arrive(0, index)
        self.pass_on(3, self.up, index)
        self.pass_on(4, self.down, index)
        index = at.head_at(dy=-1)
        self.arrive(1, index)
        self.pass_on(5, self.up, index, 0)
        index = at.head_at(dy=1)
        self.arrive(2, index)
        self.pass_on(6, self.down, index, 1)

    def third(self):
        at = self.at
        index = at.head_at(flip=True, dy=-1)
        self.arrive(3, index)
        self.pass_on(7, self.up, index, 0)
        index = at.head_at(flip=True, dy=1)
        self.arrive(4, index)
        self.pass_on(8, self.down, index, 1)

    def whole(self):
        at = self.at
        for event, flip in ((5, False), (7, True)):
            index = at.head_at(flip=flip, dy=2)
            self.arrive(event, index, 0)
            self.arrive(event + 1, index, 1)

    halves = (5, 6, 7, 8)
    events = 9
    close = Gather.close


def dot_nt(left, right):
    return lax.dot_general(
        left, right, (((1,), (1,)), ((), ())), preferred_element_type=jnp.float32
    )


def layer_kernel(
    x_ref, wk_ref, wv_ref, wq_ref, wo_ref, kern_ref, mix_ref, cos_ref, sin_ref, gain_ref, o_ref,
    x_buf, wk_buf, wq_buf, wv_buf, k_buf, v_buf, wo_buf, made, qx, rim_in,
    q32, k32, qt, kc, lg, band, ps, acc, mass, peaks, normed, part,
    y_half, y_sum, y_full, give, got,
    send, recv, x_send, x_recv, here, rim_sems, r_send, r_recv,
):
    at = Places()
    place = at.ctx
    r0 = place * ROWS
    blocks = lax.div(place + 2, 2)
    scale = 1.0 / math.sqrt(HD)
    after = {"ctx": lax.rem(at.ctx + 1, 16)}
    greet(
        [{"ctx": at.ctx_at(flip_core=True)}, {"ctx": at.ctx_at(flip_col=True)}]
        + [{"ctx": at.ctx_at(dz=1)}, {"ctx": at.ctx_at(dz=-1)}]
        + [{"head": at.head_at(dy=1)}, {"head": at.head_at(dy=-1)}, {"head": at.head_at(flip=True)}]
        + [after, {"ctx": lax.rem(at.ctx + 15, 16)}]
    )

    def gather(t, own, buf, rows, base=0):
        return Gather(at, own, buf, rows, send.at[t], recv.at[t], base)

    feats = Features(at, x_ref, x_buf, x_send, x_recv)
    wk = gather(0, wk_ref, wk_buf, ROWS)
    wv = gather(1, wv_ref, wv_buf, ROWS)
    wq = gather(2, wq_ref, wq_buf, ROWS)
    keys = gather(3, None, k_buf, ROWS, HD)
    values = gather(4, None, v_buf, ROWS)
    wo = gather(5, wo_ref, wo_buf, 2 * ROWS)
    keys.own = keys.slot(at.ctx)
    values.own = values.slot(at.ctx)

    wk.first()
    feats.first()
    own = [
        pltpu.make_async_copy(x_ref, feats.slot(at.head), here.at[0]),
        pltpu.make_async_copy(wk_ref, wk.slot(at.ctx), here.at[1]),
        pltpu.make_async_copy(wq_ref, wq.slot(at.ctx), here.at[3]),
        pltpu.make_async_copy(wv_ref, wv.slot(at.ctx), here.at[2]),
        pltpu.make_async_copy(wo_ref, wo.slot(at.ctx), here.at[4]),
    ]
    for copy in own:
        copy.start()
    k_buf[:HD] = jnp.zeros((HD, GROUP * HD), jnp.bfloat16)
    k_buf[HD + TOKENS :] = jnp.zeros((16, GROUP * HD), jnp.bfloat16)

    def project(buf):
        return jnp.dot(x_buf[...], buf[...], preferred_element_type=jnp.float32)

    def rotate(projected):
        turned = []
        for h in range(GROUP):
            piece = projected[:, h * HD : (h + 1) * HD]
            turned.append(piece * cos_ref[...] + pltpu.roll(piece, HD // 2, 1) * sin_ref[...])
        return jnp.concatenate(turned, 1)

    def keep(index, value, dst):
        made[index] = value.astype(jnp.bfloat16)
        copy = pltpu.make_async_copy(made.at[index], dst, here.at[5 + index])
        copy.start()
        copy.wait()

    wk.second()
    feats.second()
    wq.first()
    wk.third()
    feats.third()
    wq.second()
    wk.last()
    for copy in own:
        copy.wait()
    feats.whole()
    wk.whole()
    keep(0, rotate(project(wk_buf)), keys.slot(at.ctx))
    keys.first()
    wv.first()
    wq.third()
    wq.last()
    keys.second()
    wq.whole()
    keep(2, rotate(project(wq_buf)), qx.at[pl.ds(16, ROWS)])
    rim = pltpu.make_async_remote_copy(
        src_ref=qx.at[pl.ds(ROWS, 16)], dst_ref=rim_in,
        send_sem=rim_sems.at[0], recv_sem=rim_sems.at[1], device_id=after, device_id_type=MESH,
    )
    rim.start()
    wv.second()
    keys.third()
    rim.wait()
    qx[:16] = jnp.where(place > 0, rim_in[...], jnp.zeros_like(rim_in))
    for h in range(GROUP):
        q32[h] = qx[:, h * HD : (h + 1) * HD].astype(jnp.float32)[8:] * scale

    def mix_lags(r, _):
        for h in range(GROUP):
            view = q32.at[h, pl.ds(pl.multiple_of(r * 16, 16), 24)]
            lags = [view[8 - a : 24 - a] for a in range(CQ)]
            for c in range(CK):
                total = kern_ref[h, c] * lags[0]
                for a in range(1, CQ):
                    total = total + kern_ref[h, a * CK + c] * lags[a]
                qt[h, pl.ds(pl.multiple_of(r * 16, 16), 16), c * HD : (c + 1) * HD] = total.astype(
                    jnp.bfloat16
                )
        return 0

    lax.fori_loop(0, ROWS // 16, mix_lags, 0)
    keys.last()
    keys.whole()

    def value_step():
        wv.last()
        wv.whole()
        keep(1, project(wv_buf), values.slot(at.ctx))
        values.first()
        wo.first()

    steps = {1: [wv.third], 3: [value_step], 5: [values.second], 7: [wo.second, values.third]}

    def block_logits(b, _):
        for when, actions in steps.items():

            @pl.when(b == when)
            def _(actions=actions):
                for action in actions:
                    action()

        @pl.when(b < blocks)
        def _():
            for h in range(GROUP):
                rows = k_buf[pl.ds(pl.multiple_of(HD - 16 + b * KB, 16), KB + 32), h * HD : (h + 1) * HD]
                k32[h] = rows.astype(jnp.float32)
                for c in range(CK):
                    start = 16 + CK // 2 - c
                    kc[h % 2, :, c * HD : (c + 1) * HD] = k32[h, start : start + KB].astype(jnp.bfloat16)
                lg[h, :, pl.ds(pl.multiple_of(HD + b * KB, HD), KB)] = dot_nt(qt[h], kc[h % 2])

        return 0

    lax.fori_loop(0, 8, block_logits, 0)

    for s in range(2):
        for h in range(GROUP):
            cols = slice(h * HD, (h + 1) * HD)
            near = k_buf[pl.ds(pl.multiple_of(r0 + s * HD, HD), 2 * HD), cols]
            scores = dot_nt(qx[s * HD : s * HD + HD + 16, cols], near)[8:] * scale
            apart = (
                lax.broadcasted_iota(jnp.int32, scores.shape, 0)
                - lax.broadcasted_iota(jnp.int32, scores.shape, 1)
                + (HD - 8)
            )
            kept = jnp.where((apart >= 0) & (apart <= 24), scores, 0.0)
            band[s * GROUP + h, 0] = kept[:, :HD]
            band[s * GROUP + h, 1] = kept[:, HD:]

    row_in = lax.broadcasted_iota(jnp.int32, (8, HD), 0)
    col_in = lax.broadcasted_iota(jnp.int32, (8, HD), 1)

    def taps(h, lags, width):
        total = None
        for c in range(CK):
            piece = kern_ref[h, c] * lags[0]
            for a in range(1, CQ):
                piece = piece + kern_ref[h, a * CK + c] * lags[a]
            shift = (c - CK // 2) % width
            piece = pltpu.roll(piece, shift, 1) if shift else piece
            total = piece if total is None else total + piece
        return total

    def two_tiles(k, _):
        for s in range(2):
            here_cols = pl.ds(pl.multiple_of(HD + r0 + s * HD, HD), HD)
            prior = pl.ds(pl.multiple_of(r0 + s * HD, HD), HD)
            for h in range(GROUP):
                views = [
                    band.at[s * GROUP + h, t, pl.ds(pl.multiple_of(8 * k, 8), 16)] for t in range(2)
                ]
                lags = [
                    jnp.concatenate([view[8 - a : 16 - a] for view in views], 1) for a in range(CQ)
                ]
                direct = taps(h, lags, 2 * HD)
                rows = pl.ds(pl.multiple_of(s * HD + 8 * k, 8), 8)
                apart = 8 * k + row_in - col_in
                lg[h, rows, prior] = jnp.where(
                    apart + HD >= BAND, lg[h, rows, prior], direct[:, :HD]
                )
                lg[h, rows, here_cols] = jnp.where(
                    apart >= BAND,
                    lg[h, rows, here_cols],
                    jnp.where(apart >= 0, direct[:, HD:], -jnp.inf),
                )
        return 0

    def one_tile(k, _):
        for s in range(2):
            here_cols = pl.ds(pl.multiple_of(HD + r0 + s * HD, HD), HD)
            for h in range(GROUP):
                view = band.at[s * GROUP + h, 1, pl.ds(pl.multiple_of(8 * k, 8), 16)]
                direct = taps(h, [view[8 - a : 16 - a] for a in range(CQ)], HD)
                rows = pl.ds(pl.multiple_of(s * HD + 8 * k, 8), 8)
                apart = 8 * k + row_in - col_in
                lg[h, rows, here_cols] = jnp.where(
                    apart >= BAND,
                    lg[h, rows, here_cols],
                    jnp.where(apart >= 0, direct, -jnp.inf),
                )
        return 0

    lax.fori_loop(0, 2, two_tiles, 0)
    lax.fori_loop(2, HD // 8, one_tile, 0)
    for h in range(GROUP):
        lg[h, :HD, pl.ds(pl.multiple_of(2 * HD + r0, HD), HD)] = jnp.full(
            (HD, HD), -jnp.inf, jnp.float32
        )

    @pl.when(lax.rem(place, 2) == 0)
    def _():
        for h in range(GROUP):
            lg[h, :, pl.ds(pl.multiple_of(3 * HD + r0, HD), ROWS)] = jnp.full(
                (ROWS, ROWS), -jnp.inf, jnp.float32
            )

    for g in range(GROUP):

        def peak_of(b, peak, g=g):
            block = lg[g, :, pl.ds(pl.multiple_of(HD + b * KB, HD), KB)]
            for t in range(KB // HD):
                peak = jnp.maximum(peak, block[:, t * HD : (t + 1) * HD])
            return peak

        peak = lax.fori_loop(0, blocks, peak_of, jnp.full((ROWS, HD), -jnp.inf, jnp.float32))
        peaks[g] = jnp.broadcast_to(jnp.max(peak, axis=1, keepdims=True), (ROWS, HD))

    values.last()
    wo.third()
    values.whole()

    up = {"head": at.head_at(dy=1)}
    down = {"head": at.head_at(dy=-1)}
    partner = {"head": at.head_at(flip=True)}
    quarter = HALF // 2
    y_up, y_down, y_far = (lax.rem(at.y + d, 4) for d in (1, 3, 2))

    def ring_copy(r, event):
        top, low = pl.ds(0, quarter), pl.ds(quarter, quarter)
        target, src, dst = (
            (up, part.at[r, y_far, :, top], y_half.at[r, 0]),
            (down, part.at[r, y_far, :, low], y_half.at[r, 1]),
            (up, y_sum.at[r, 0], y_full.at[r, 0]),
            (down, y_sum.at[r, 1], y_full.at[r, 1]),
            (partner, give.at[r], got.at[r]),
        )[event]
        return pltpu.make_async_remote_copy(
            src_ref=src, dst_ref=dst, send_sem=r_send.at[r, event], recv_sem=r_recv.at[r, event],
            device_id=target, device_id_type=MESH,
        )

    def add(left, right):
        return (left.astype(jnp.float32) + right.astype(jnp.float32)).astype(jnp.bfloat16)

    def ring_first(r):
        ring_copy(r, 0).start()
        ring_copy(r, 1).start()
        y_sum[r, 0, :, quarter:] = part[r, y_up, :, quarter:]
        y_sum[r, 1, :, :quarter] = part[r, y_down, :, :quarter]

    def ring_second(r):
        ring_copy(r, 0).wait_recv()
        y_sum[r, 0, :, :quarter] = add(part[r, y_up, :, :quarter], y_half[r, 0])
        ring_copy(r, 2).start()
        ring_copy(r, 1).wait_recv()
        y_sum[r, 1, :, quarter:] = add(part[r, y_down, :, quarter:], y_half[r, 1])
        ring_copy(r, 3).start()

    def ring_total(r, far):
        return (
            part[r, at.y, far].astype(jnp.float32)
            + y_full[r, 0, far].astype(jnp.float32)
            + y_full[r, 1, far].astype(jnp.float32)
        )

    def ring_third(r):
        ring_copy(r, 2).wait_recv()
        ring_copy(r, 3).wait_recv()
        give[r] = ring_total(r, 1 - at.far).astype(jnp.bfloat16)
        ring_copy(r, 4).start()

    def ring_last(r):
        mine = ring_total(r, at.far)
        ring_copy(r, 4).wait_recv()
        total = mine + got[r].astype(jnp.float32)
        o_ref[r * HALF : (r + 1) * HALF] = total.astype(jnp.bfloat16)

    for r in range(2):
        rows = slice(r * HALF, (r + 1) * HALF)
        acc[...] = jnp.zeros_like(acc)
        mass[...] = jnp.zeros_like(mass)

        def weigh(b, _, r=r, rows=rows):
            if r == 1:
                pl.when(b == 2)(lambda: ring_second(0))
                pl.when(b == 5)(lambda: ring_third(0))

            @pl.when(b < blocks)
            def _():
                for g in range(GROUP):
                    peak = peaks[g, rows]
                    total = mass[g]
                    for t in range(KB // HD):
                        block = lg[g, rows, pl.ds(pl.multiple_of(HD + b * KB + t * HD, HD), HD)]
                        probs = jnp.exp(block - peak)
                        total = total + probs
                        ps[g * HALF : (g + 1) * HALF, t * HD : (t + 1) * HD] = probs.astype(jnp.bfloat16)
                    mass[g] = total
                block = v_buf[pl.ds(pl.multiple_of(b * KB, KB), KB), :]
                acc[...] += jnp.dot(ps[...], block, preferred_element_type=jnp.float32)

            return 0

        lax.fori_loop(0, 8, weigh, 0)
        inverse = [
            jnp.broadcast_to(1.0 / jnp.sum(mass[g], axis=1, keepdims=True), (HALF, HD))
            for g in range(GROUP)
        ]
        for h in range(GROUP):
            cols = slice(h * HD, (h + 1) * HD)
            total = mix_ref[h, 0] * (acc[:HALF, cols] * inverse[0])
            for g in range(1, GROUP):
                total = total + mix_ref[h, g] * (acc[g * HALF : (g + 1) * HALF, cols] * inverse[g])
            rms = jnp.sqrt(jnp.mean(total * total, axis=1, keepdims=True) + 1e-05)
            normed[:, cols] = (total / rms * gain_ref[:, cols]).astype(jnp.bfloat16)
        if r == 0:
            wo.last()
            wo.whole()

        def out_block(b, _, r=r):
            width = GROUP * HD
            source = pl.ds(pl.multiple_of(b * width, width), width)
            piece = jnp.dot(normed[...], wo_buf[source], preferred_element_type=jnp.float32)
            far, y, side = lax.div(b, 8), lax.rem(lax.div(b, 2), 4), lax.rem(b, 2)
            part[r, y, far, :, pl.ds(pl.multiple_of(side * ROWS, ROWS), ROWS)] = piece.astype(jnp.bfloat16)
            return 0

        lax.fori_loop(0, 16, out_block, 0)
        ring_first(r)

    ring_last(0)
    ring_second(1)
    ring_third(1)
    ring_last(1)
    for r in range(2):
        for event in range(5):
            ring_copy(r, event).wait_send()
    for each in (feats, wk, wv, wq, keys, values, wo):
        each.close()


def layer(*operands):
    smem = pl.BlockSpec(memory_space=pltpu.SMEM)
    vmem = pl.BlockSpec(memory_space=pltpu.VMEM)
    hbm = pl.BlockSpec(memory_space=pltpu.HBM)
    width = GROUP * HD
    half = lambda *dims: pltpu.VMEM(dims, jnp.bfloat16)
    full = lambda *dims: pltpu.VMEM(dims, jnp.float32)
    dma = pltpu.SemaphoreType.DMA
    return pl.pallas_call(
        layer_kernel,
        out_shape=jax.ShapeDtypeStruct((ROWS, width), jnp.bfloat16),
        in_specs=[hbm] * 5 + [smem] * 2 + [vmem] * 3,
        out_specs=vmem,
        scratch_shapes=[
            half(ROWS, TOKENS), half(TOKENS, width), half(TOKENS, width), half(TOKENS, width),
            half(HD + TOKENS + 16, width), half(TOKENS, width), half(16 * width, ROWS),
            half(3, ROWS, width), half(ROWS + 16, width), half(16, width),
            full(GROUP, ROWS + 8, HD), full(GROUP, KB + 32, HD),
            half(GROUP, ROWS, CK * HD), half(2, KB, CK * HD),
            full(GROUP, ROWS, HD + TOKENS), full(2 * GROUP, 2, HD + 8, HD),
            half(GROUP * HALF, KB), full(GROUP * HALF, width),
            full(GROUP, HALF, HD), full(GROUP, ROWS, HD), half(HALF, width),
            half(2, 4, 2, HALF, width),
            half(2, 2, 2, HALF // 2, width), half(2, 2, 2, HALF, width), half(2, 2, 2, HALF, width),
            half(2, HALF, width), half(2, HALF, width),
            dma((6, 16)), dma((6, 16)), dma((9,)), dma((9,)), dma((8,)), dma((2,)), dma((2, 5)), dma((2, 5)),
        ],
        compiler_params=pltpu.CompilerParams(
            collective_id=1, has_side_effects=True, vmem_limit_bytes=67043328
        ),
        name="layer",
    )(*operands)


def per_device(
    activations, positions, w_query, w_key, w_value, conv_kernel, head_mix, out_gain, w_out
):
    exponents = jnp.arange(HD // 2, dtype=jnp.float32) * (2.0 / HD)
    inverse = jnp.exp(-exponents * math.log(500000.0))
    angle = (positions.astype(jnp.float32) * 0.25)[:, None] * inverse[None, :]
    cosine = jnp.cos(angle)
    sine = jnp.sin(angle)
    return layer(
        activations, w_key, w_value, w_query, w_out, conv_kernel, head_mix,
        jnp.concatenate([cosine, cosine], 1), jnp.concatenate([-sine, sine], 1),
        out_gain.reshape(1, -1),
    )


def solution(mesh):
    return jax.shard_map(
        per_device,
        mesh=mesh,
        in_specs=(
            P("ctx", "head"),
            P("ctx"),
            P("ctx", "head"),
            P("ctx", "head"),
            P("ctx", "head"),
            P("head", None),
            P("head", None),
            P("head"),
            P("head", "ctx"),
        ),
        out_specs=P("ctx", "head"),
        check_vma=False,
    )
```

time: 206 us -> 168 us (0.82); the launches traced: 206 us -> 165 us
  Pallas kernels: 190 us -> 161 us
  local copies, waits for them, and re-layouts: 14.2 us -> 2.34 us
    pallas_call x3 -> x1, Pallas kernels: 190 us -> 161 us  [layer(): pl.pallas_call(layer_kernel, out_shape=jax.ShapeDtypeStruct((ROWS, width)...]
    unnamed x23 -> x3, local copies, waits for them, and re-layouts: 14.2 us -> 2.34 us
where the time goes in v3:
time: 168 us; the launch traced here: 165 us
  Pallas kernels  161 us (96%)
  local copies, waits for them, and re-layouts  2.34 us (1%)
    pallas_call x1, Pallas kernels, layer(): pl.pallas_call(layer_kernel, out_shape=jax.ShapeDtypeStruct((ROWS, width)...  161 us

profile of v3, /device:TPU:98, one launch (start us, length us, event | category | flops | bytes accessed | tf_op | source)
XLA Modules:
  0.0 164.8 jit_solution(5302188999378365611)
XLA Ops:
  0.0 0.0 copy-start
  0.0 0.7 copy-done
  0.7 0.5 fusion
  1.2 0.9 pad_maximum_fusion
  2.1 161.0 %layer.1 = bf16[256,512]{1,0:T(8,128)(2,1)} custom-call(bf16[256,512]{1,0:T(8,128)(2,1)} %x_ref.1, bf16[256,512]{1,0:T(8,128)(2,1)} %wk_ref.1, bf16[256,512]{1,0:T(8,128)(2,1)} %wv_ref.1, bf16[256,512]{1,0:T(8,128)(2,1)} %wq_ref.1, bf16[512,256]{1,0:T(8,128)(2,1)} %wo_ref.1, f32[4,66]{1,0:T(4,128)} %kern_ref.1, f32[4,4]{1,0:T(4,128)} %mix_ref.1, ...), custom_call_target="tpu_custom_call" | custom-call | tf_op jit(solution)/shard_map/layer/pallas_call | solution.py:578
  163.1 1.7 %copy.11 = bf16[256,512]{1,0:T(8,128)(2,1)} copy(bf16[256,512]{1,0:T(8,128)(2,1)} %layer.1) | data formatting | bytes 524288
  (2 shorter events, 0.0 us)
Async XLA Ops:
  0.0 0.7 copy-start

commit v4 on v3

--- a/solution.py
+++ b/solution.py
@@ -45,7 +45,7 @@
     barrier = pltpu.get_barrier_semaphore()
     for target in targets:
         pl.semaphore_signal(barrier, inc=1, device_id=target, device_id_type=MESH)
-    pl.semaphore_wait(barrier, len(targets))
+    return lambda: pl.semaphore_wait(barrier, len(targets))
 
 
 class Gather:
@@ -211,8 +211,8 @@
 
 def layer_kernel(
     x_ref, wk_ref, wv_ref, wq_ref, wo_ref, kern_ref, mix_ref, cos_ref, sin_ref, gain_ref, o_ref,
-    x_buf, wk_buf, wq_buf, wv_buf, k_buf, v_buf, wo_buf, made, qx, rim_in,
-    q32, k32, qt, kc, lg, band, ps, acc, mass, peaks, normed, part,
+    x_buf, w_buf, wv_buf, k_buf, v_buf, wo_buf, made, qx, rim_in,
+    q32, k32, qt, kc, lg, band, acc, mass, peaks, normed, part,
     y_half, y_sum, y_full, give, got,
     send, recv, x_send, x_recv, here, rim_sems, r_send, r_recv,
 ):
@@ -222,7 +222,7 @@
     blocks = lax.div(place + 2, 2)
     scale = 1.0 / math.sqrt(HD)
     after = {"ctx": lax.rem(at.ctx + 1, 16)}
-    greet(
+    met = greet(
         [{"ctx": at.ctx_at(flip_core=True)}, {"ctx": at.ctx_at(flip_col=True)}]
         + [{"ctx": at.ctx_at(dz=1)}, {"ctx": at.ctx_at(dz=-1)}]
         + [{"head": at.head_at(dy=1)}, {"head": at.head_at(dy=-1)}, {"head": at.head_at(flip=True)}]
@@ -233,17 +233,15 @@
         return Gather(at, own, buf, rows, send.at[t], recv.at[t], base)
 
     feats = Features(at, x_ref, x_buf, x_send, x_recv)
-    wk = gather(0, wk_ref, wk_buf, ROWS)
+    wk = gather(0, wk_ref, w_buf, ROWS)
     wv = gather(1, wv_ref, wv_buf, ROWS)
-    wq = gather(2, wq_ref, wq_buf, ROWS)
+    wq = gather(2, wq_ref, w_buf, ROWS, TOKENS)
     keys = gather(3, None, k_buf, ROWS, HD)
     values = gather(4, None, v_buf, ROWS)
     wo = gather(5, wo_ref, wo_buf, 2 * ROWS)
     keys.own = keys.slot(at.ctx)
     values.own = values.slot(at.ctx)
 
-    wk.first()
-    feats.first()
     own = [
         pltpu.make_async_copy(x_ref, feats.slot(at.head), here.at[0]),
         pltpu.make_async_copy(wk_ref, wk.slot(at.ctx), here.at[1]),
@@ -256,8 +254,12 @@
     k_buf[:HD] = jnp.zeros((HD, GROUP * HD), jnp.bfloat16)
     k_buf[HD + TOKENS :] = jnp.zeros((16, GROUP * HD), jnp.bfloat16)
 
+    met()
+    wk.first()
+    feats.first()
+
     def project(buf):
-        return jnp.dot(x_buf[...], buf[...], preferred_element_type=jnp.float32)
+        return jnp.dot(x_buf[...], buf[:TOKENS], preferred_element_type=jnp.float32)
 
     def rotate(projected):
         turned = []
@@ -278,26 +280,27 @@
     wk.third()
     feats.third()
     wq.second()
+    wv.first()
     wk.last()
     for copy in own:
         copy.wait()
     feats.whole()
     wk.whole()
-    keep(0, rotate(project(wk_buf)), keys.slot(at.ctx))
+    keep(0, rotate(project(w_buf.at[:TOKENS])), keys.slot(at.ctx))
+    wq.third()
     keys.first()
-    wv.first()
-    wq.third()
+    wv.second()
     wq.last()
-    keys.second()
     wq.whole()
-    keep(2, rotate(project(wq_buf)), qx.at[pl.ds(16, ROWS)])
+    keep(2, rotate(project(w_buf.at[TOKENS:])), qx.at[pl.ds(16, ROWS)])
     rim = pltpu.make_async_remote_copy(
         src_ref=qx.at[pl.ds(ROWS, 16)], dst_ref=rim_in,
         send_sem=rim_sems.at[0], recv_sem=rim_sems.at[1], device_id=after, device_id_type=MESH,
     )
     rim.start()
-    wv.second()
-    keys.third()
+    keys.second()
+    wv.third()
+    wo.first()
     rim.wait()
     qx[:16] = jnp.where(place > 0, rim_in[...], jnp.zeros_like(rim_in))
     for h in range(GROUP):
@@ -316,18 +319,17 @@
                 )
         return 0
 
+    keys.third()
     lax.fori_loop(0, ROWS // 16, mix_lags, 0)
+    wv.last()
     keys.last()
+    wv.whole()
+    keep(1, project(wv_buf), values.slot(at.ctx))
+    values.first()
+    wo.second()
     keys.whole()
 
-    def value_step():
-        wv.last()
-        wv.whole()
-        keep(1, project(wv_buf), values.slot(at.ctx))
-        values.first()
-        wo.first()
-
-    steps = {1: [wv.third], 3: [value_step], 5: [values.second], 7: [wo.second, values.third]}
+    steps = {1: [values.second], 2: [wo.third], 4: [values.third], 6: [wo.last]}
 
     def block_logits(b, _):
         for when, actions in steps.items():
@@ -350,6 +352,7 @@
         return 0
 
     lax.fori_loop(0, 8, block_logits, 0)
+    values.last()
 
     for s in range(2):
         for h in range(GROUP):
@@ -443,21 +446,41 @@
         peak = lax.fori_loop(0, blocks, peak_of, jnp.full((ROWS, HD), -jnp.inf, jnp.float32))
         peaks[g] = jnp.broadcast_to(jnp.max(peak, axis=1, keepdims=True), (ROWS, HD))
 
-    values.last()
-    wo.third()
+    wk.close()
+    wq.close()
+    mass[...] = jnp.zeros_like(mass)
+
+    def raise_block(b, _):
+        for g in range(GROUP):
+            for r in range(2):
+                rows = slice(r * HALF, (r + 1) * HALF)
+                peak = peaks[g, rows]
+                total = mass[g, rows]
+                first = b * GROUP * ROWS + (r * GROUP + g) * HALF
+                for t in range(KB // HD):
+                    block = lg[g, rows, pl.ds(pl.multiple_of(HD + b * KB + t * HD, HD), HD)]
+                    probs = jnp.exp(block - peak)
+                    total = total + probs
+                    w_buf[pl.ds(pl.multiple_of(first, HALF), HALF), t * HD : (t + 1) * HD] = probs.astype(
+                        jnp.bfloat16
+                    )
+                mass[g, rows] = total
+        return 0
+
+    lax.fori_loop(0, blocks, raise_block, 0)
     values.whole()
 
     up = {"head": at.head_at(dy=1)}
     down = {"head": at.head_at(dy=-1)}
     partner = {"head": at.head_at(flip=True)}
-    quarter = HALF // 2
+    chunk = ROWS // 4
+    quarter = chunk // 2
     y_up, y_down, y_far = (lax.rem(at.y + d, 4) for d in (1, 3, 2))
 
     def ring_copy(r, event):
-        top, low = pl.ds(0, quarter), pl.ds(quarter, quarter)
         target, src, dst = (
-            (up, part.at[r, y_far, :, top], y_half.at[r, 0]),
-            (down, part.at[r, y_far, :, low], y_half.at[r, 1]),
+            (up, part.at[y_far, :, pl.ds(r * chunk, quarter)], y_half.at[r, 0]),
+            (down, part.at[y_far, :, pl.ds(r * chunk + quarter, quarter)], y_half.at[r, 1]),
             (up, y_sum.at[r, 0], y_full.at[r, 0]),
             (down, y_sum.at[r, 1], y_full.at[r, 1]),
             (partner, give.at[r], got.at[r]),
@@ -473,20 +496,20 @@
     def ring_first(r):
         ring_copy(r, 0).start()
         ring_copy(r, 1).start()
-        y_sum[r, 0, :, quarter:] = part[r, y_up, :, quarter:]
-        y_sum[r, 1, :, :quarter] = part[r, y_down, :, :quarter]
+        y_sum[r, 0, :, quarter:] = part[y_up, :, r * chunk + quarter : (r + 1) * chunk]
+        y_sum[r, 1, :, :quarter] = part[y_down, :, r * chunk : r * chunk + quarter]
 
     def ring_second(r):
         ring_copy(r, 0).wait_recv()
-        y_sum[r, 0, :, :quarter] = add(part[r, y_up, :, :quarter], y_half[r, 0])
+        y_sum[r, 0, :, :quarter] = add(part[y_up, :, r * chunk : r * chunk + quarter], y_half[r, 0])
         ring_copy(r, 2).start()
         ring_copy(r, 1).wait_recv()
-        y_sum[r, 1, :, quarter:] = add(part[r, y_down, :, quarter:], y_half[r, 1])
+        y_sum[r, 1, :, quarter:] = add(part[y_down, :, r * chunk + quarter : (r + 1) * chunk], y_half[r, 1])
         ring_copy(r, 3).start()
 
     def ring_total(r, far):
         return (
-            part[r, at.y, far].astype(jnp.float32)
+            part[at.y, far, r * chunk : (r + 1) * chunk].astype(jnp.float32)
             + y_full[r, 0, far].astype(jnp.float32)
             + y_full[r, 1, far].astype(jnp.float32)
         )
@@ -501,37 +524,22 @@
         mine = ring_total(r, at.far)
         ring_copy(r, 4).wait_recv()
         total = mine + got[r].astype(jnp.float32)
-        o_ref[r * HALF : (r + 1) * HALF] = total.astype(jnp.bfloat16)
+        o_ref[r * chunk : (r + 1) * chunk] = total.astype(jnp.bfloat16)
 
     for r in range(2):
         rows = slice(r * HALF, (r + 1) * HALF)
         acc[...] = jnp.zeros_like(acc)
-        mass[...] = jnp.zeros_like(mass)
-
-        def weigh(b, _, r=r, rows=rows):
-            if r == 1:
-                pl.when(b == 2)(lambda: ring_second(0))
-                pl.when(b == 5)(lambda: ring_third(0))
-
-            @pl.when(b < blocks)
-            def _():
-                for g in range(GROUP):
-                    peak = peaks[g, rows]
-                    total = mass[g]
-                    for t in range(KB // HD):
-                        block = lg[g, rows, pl.ds(pl.multiple_of(HD + b * KB + t * HD, HD), HD)]
-                        probs = jnp.exp(block - peak)
-                        total = total + probs
-                        ps[g * HALF : (g + 1) * HALF, t * HD : (t + 1) * HD] = probs.astype(jnp.bfloat16)
-                    mass[g] = total
-                block = v_buf[pl.ds(pl.multiple_of(b * KB, KB), KB), :]
-                acc[...] += jnp.dot(ps[...], block, preferred_element_type=jnp.float32)
-
+
+        def weigh(b, _, r=r):
+            first = b * GROUP * ROWS + r * GROUP * HALF
+            left = w_buf[pl.ds(pl.multiple_of(first, HALF), GROUP * HALF)]
+            block = v_buf[pl.ds(pl.multiple_of(b * KB, KB), KB), :]
+            acc[...] += jnp.dot(left, block, preferred_element_type=jnp.float32)
             return 0
 
-        lax.fori_loop(0, 8, weigh, 0)
+        lax.fori_loop(0, blocks, weigh, 0)
         inverse = [
-            jnp.broadcast_to(1.0 / jnp.sum(mass[g], axis=1, keepdims=True), (HALF, HD))
+            jnp.broadcast_to(1.0 / jnp.sum(mass[g, rows], axis=1, keepdims=True), (HALF, HD))
             for g in range(GROUP)
         ]
         for h in range(GROUP):
@@ -540,30 +548,45 @@
             for g in range(1, GROUP):
                 total = total + mix_ref[h, g] * (acc[g * HALF : (g + 1) * HALF, cols] * inverse[g])
             rms = jnp.sqrt(jnp.mean(total * total, axis=1, keepdims=True) + 1e-05)
-            normed[:, cols] = (total / rms * gain_ref[:, cols]).astype(jnp.bfloat16)
-        if r == 0:
-            wo.last()
-            wo.whole()
-
-        def out_block(b, _, r=r):
+            normed[rows, cols] = (total / rms * gain_ref[:, cols]).astype(jnp.bfloat16)
+
+    wo.whole()
+
+    def project_out(r):
+        rows = slice(r * HALF, (r + 1) * HALF)
+
+        def out_block(b, _):
             width = GROUP * HD
             source = pl.ds(pl.multiple_of(b * width, width), width)
-            piece = jnp.dot(normed[...], wo_buf[source], preferred_element_type=jnp.float32)
+            piece = jnp.dot(normed[rows], wo_buf[source], preferred_element_type=jnp.float32)
             far, y, side = lax.div(b, 8), lax.rem(lax.div(b, 2), 4), lax.rem(b, 2)
-            part[r, y, far, :, pl.ds(pl.multiple_of(side * ROWS, ROWS), ROWS)] = piece.astype(jnp.bfloat16)
+            part[y, far, rows, pl.ds(pl.multiple_of(side * ROWS, ROWS), ROWS)] = piece.astype(jnp.bfloat16)
             return 0
 
         lax.fori_loop(0, 16, out_block, 0)
-        ring_first(r)
-
+
+    project_out(0)
+    ring_first(0)
+    ring_first(1)
+    project_out(1)
+    ring_first(2)
+    ring_second(0)
+    ring_first(3)
+    ring_second(1)
+    ring_third(0)
+    ring_second(2)
+    ring_third(1)
+    ring_second(3)
+    ring_third(2)
     ring_last(0)
-    ring_second(1)
-    ring_third(1)
     ring_last(1)
-    for r in range(2):
+    ring_third(3)
+    ring_last(2)
+    ring_last(3)
+    for r in range(4):
         for event in range(5):
             ring_copy(r, event).wait_send()
-    for each in (feats, wk, wv, wq, keys, values, wo):
+    for each in (feats, wv, keys, values, wo):
         each.close()
 
 
@@ -581,18 +604,18 @@
         in_specs=[hbm] * 5 + [smem] * 2 + [vmem] * 3,
         out_specs=vmem,
         scratch_shapes=[
-            half(ROWS, TOKENS), half(TOKENS, width), half(TOKENS, width), half(TOKENS, width),
+            half(ROWS, TOKENS), half(2 * TOKENS, width), half(TOKENS, width),
             half(HD + TOKENS + 16, width), half(TOKENS, width), half(16 * width, ROWS),
             half(3, ROWS, width), half(ROWS + 16, width), half(16, width),
             full(GROUP, ROWS + 8, HD), full(GROUP, KB + 32, HD),
             half(GROUP, ROWS, CK * HD), half(2, KB, CK * HD),
             full(GROUP, ROWS, HD + TOKENS), full(2 * GROUP, 2, HD + 8, HD),
-            half(GROUP * HALF, KB), full(GROUP * HALF, width),
-            full(GROUP, HALF, HD), full(GROUP, ROWS, HD), half(HALF, width),
-            half(2, 4, 2, HALF, width),
-            half(2, 2, 2, HALF // 2, width), half(2, 2, 2, HALF, width), half(2, 2, 2, HALF, width),
-            half(2, HALF, width), half(2, HALF, width),
-            dma((6, 16)), dma((6, 16)), dma((9,)), dma((9,)), dma((8,)), dma((2,)), dma((2, 5)), dma((2, 5)),
+            full(GROUP * HALF, width),
+            full(GROUP, ROWS, HD), full(GROUP, ROWS, HD), half(ROWS, width),
+            half(4, 2, ROWS, width),
+            half(4, 2, 2, ROWS // 8, width), half(4, 2, 2, ROWS // 4, width), half(4, 2, 2, ROWS // 4, width),
+            half(4, ROWS // 4, width), half(4, ROWS // 4, width),
+            dma((6, 16)), dma((6, 16)), dma((9,)), dma((9,)), dma((8,)), dma((2,)), dma((4, 5)), dma((4, 5)),
         ],
         compiler_params=pltpu.CompilerParams(
             collective_id=1, has_side_effects=True, vmem_limit_bytes=67043328

time: 168 us -> 159 us (0.946); the launches traced: 165 us -> 159 us
  Pallas kernels: 161 us -> 155 us
    pallas_call x1, Pallas kernels: 161 us -> 155 us  [layer(): pl.pallas_call(layer_kernel, out_shape=jax.ShapeDtypeStruct((ROWS, width)...]
where the time goes in v4:
time: 159 us
  Pallas kernels  155 us (97%)
  local copies, waits for them, and re-layouts  2.34 us (1%)
    pallas_call x1, Pallas kernels, layer(): pl.pallas_call(layer_kernel, out_shape=jax.ShapeDtypeStruct((ROWS, width)...  155 us

profile of v4, /device:TPU:98, one launch (start us, length us, event | category | flops | bytes accessed | tf_op | source)
XLA Modules:
  0.0 158.8 jit_solution(5120307024854652257)
XLA Ops:
  0.0 0.0 copy-start
  0.0 0.7 copy-done
  0.7 0.5 fusion
  1.2 0.9 pad_maximum_fusion
  2.1 155.0 %layer.1 = bf16[256,512]{1,0:T(8,128)(2,1)} custom-call(bf16[256,512]{1,0:T(8,128)(2,1)} %x_ref.1, bf16[256,512]{1,0:T(8,128)(2,1)} %wk_ref.1, bf16[256,512]{1,0:T(8,128)(2,1)} %wv_ref.1, bf16[256,512]{1,0:T(8,128)(2,1)} %wq_ref.1, bf16[512,256]{1,0:T(8,128)(2,1)} %wo_ref.1, f32[4,66]{1,0:T(4,128)} %kern_ref.1, f32[4,4]{1,0:T(4,128)} %mix_ref.1, ...), custom_call_target="tpu_custom_call" | custom-call | tf_op jit(solution)/shard_map/layer/pallas_call | solution.py:601
  157.1 1.7 %copy.11 = bf16[256,512]{1,0:T(8,128)(2,1)} copy(bf16[256,512]{1,0:T(8,128)(2,1)} %layer.1) | data formatting | bytes 524288
  (2 shorter events, 0.0 us)
Async XLA Ops:
  0.0 0.7 copy-start

commit v5 on v4

--- a/solution.py
+++ b/solution.py
@@ -329,7 +329,7 @@
     wo.second()
     keys.whole()
 
-    steps = {1: [values.second], 2: [wo.third], 4: [values.third], 6: [wo.last]}
+    steps = {2: [values.second], 5: [wo.third]}
 
     def block_logits(b, _):
         for when, actions in steps.items():
@@ -352,7 +352,7 @@
         return 0
 
     lax.fori_loop(0, 8, block_logits, 0)
-    values.last()
+    values.third()
 
     for s in range(2):
         for h in range(GROUP):
@@ -435,6 +435,7 @@
                 (ROWS, ROWS), -jnp.inf, jnp.float32
             )
 
+    values.last()
     for g in range(GROUP):
 
         def peak_of(b, peak, g=g):
@@ -468,6 +469,7 @@
         return 0
 
     lax.fori_loop(0, blocks, raise_block, 0)
+    wo.last()
     values.whole()
 
     up = {"head": at.head_at(dy=1)}
@@ -496,10 +498,10 @@
     def ring_first(r):
         ring_copy(r, 0).start()
         ring_copy(r, 1).start()
+
+    def ring_second(r):
         y_sum[r, 0, :, quarter:] = part[y_up, :, r * chunk + quarter : (r + 1) * chunk]
         y_sum[r, 1, :, :quarter] = part[y_down, :, r * chunk : r * chunk + quarter]
-
-    def ring_second(r):
         ring_copy(r, 0).wait_recv()
         y_sum[r, 0, :, :quarter] = add(part[y_up, :, r * chunk : r * chunk + quarter], y_half[r, 0])
         ring_copy(r, 2).start()
@@ -552,35 +554,29 @@
 
     wo.whole()
 
-    def project_out(r):
-        rows = slice(r * HALF, (r + 1) * HALF)
-
-        def out_block(b, _):
-            width = GROUP * HD
-            source = pl.ds(pl.multiple_of(b * width, width), width)
-            piece = jnp.dot(normed[rows], wo_buf[source], preferred_element_type=jnp.float32)
-            far, y, side = lax.div(b, 8), lax.rem(lax.div(b, 2), 4), lax.rem(b, 2)
-            part[y, far, rows, pl.ds(pl.multiple_of(side * ROWS, ROWS), ROWS)] = piece.astype(jnp.bfloat16)
-            return 0
-
-        lax.fori_loop(0, 16, out_block, 0)
-
+    def project_out(step):
+        y = lax.rem(at.y + step, 4)
+        for far in range(2):
+            for side in range(2):
+                first = (far * 8 + y * 2 + side) * GROUP * HD
+                source = pl.ds(pl.multiple_of(first, GROUP * HD), GROUP * HD)
+                piece = jnp.dot(normed[...], wo_buf[source], preferred_element_type=jnp.float32)
+                part[y, far, :, side * ROWS : (side + 1) * ROWS] = piece.astype(jnp.bfloat16)
+
+    project_out(2)
+    for r in range(4):
+        ring_first(r)
+    project_out(1)
+    project_out(3)
+    for r in range(4):
+        ring_second(r)
     project_out(0)
-    ring_first(0)
-    ring_first(1)
-    project_out(1)
-    ring_first(2)
-    ring_second(0)
-    ring_first(3)
-    ring_second(1)
     ring_third(0)
-    ring_second(2)
     ring_third(1)
-    ring_second(3)
     ring_third(2)
     ring_last(0)
+    ring_third(3)
     ring_last(1)
-    ring_third(3)
     ring_last(2)
     ring_last(3)
     for r in range(4):

time: 159 us -> 145 us (0.912)
  Pallas kernels: 155 us -> 142 us
    pallas_call x1, Pallas kernels: 155 us -> 142 us  [layer(): pl.pallas_call(layer_kernel, out_shape=jax.ShapeDtypeStruct((ROWS, width)...]
where the time goes in v5:
time: 145 us
  Pallas kernels  142 us (98%)
  local copies, waits for them, and re-layouts  2.34 us (2%)
    pallas_call x1, Pallas kernels, layer(): pl.pallas_call(layer_kernel, out_shape=jax.ShapeDtypeStruct((ROWS, width)...  142 us

profile of v5, /device:TPU:98, one launch (start us, length us, event | category | flops | bytes accessed | tf_op | source)
XLA Modules:
  0.0 145.3 jit_solution(5856983692270688687)
XLA Ops:
  0.0 0.0 copy-start
  0.0 0.7 copy-done
  0.7 0.5 fusion
  1.2 0.9 pad_maximum_fusion
  2.1 141.5 %layer.1 = bf16[256,512]{1,0:T(8,128)(2,1)} custom-call(bf16[256,512]{1,0:T(8,128)(2,1)} %x_ref.1, bf16[256,512]{1,0:T(8,128)(2,1)} %wk_ref.1, bf16[256,512]{1,0:T(8,128)(2,1)} %wv_ref.1, bf16[256,512]{1,0:T(8,128)(2,1)} %wq_ref.1, bf16[512,256]{1,0:T(8,128)(2,1)} %wo_ref.1, f32[4,66]{1,0:T(4,128)} %kern_ref.1, f32[4,4]{1,0:T(4,128)} %mix_ref.1, ...), custom_call_target="tpu_custom_call" | custom-call | tf_op jit(solution)/shard_map/layer/pallas_call | solution.py:597
  143.6 1.7 %copy.11 = bf16[256,512]{1,0:T(8,128)(2,1)} copy(bf16[256,512]{1,0:T(8,128)(2,1)} %layer.1) | data formatting | bytes 524288
  (2 shorter events, 0.0 us)
Async XLA Ops:
  0.0 0.7 copy-start

commit v6 on v5

--- a/solution.py
+++ b/solution.py
@@ -58,13 +58,17 @@
         self.down = {"ctx": at.ctx_at(dz=-1)}
 
     def slot(self, index, half=None):
-        size = self.rows if half is None else self.rows // 2
-        first = self.base + index * self.rows + (size if half == 1 else 0)
-        return self.buf.at[pl.ds(pl.multiple_of(first, 128), size), :]
+        short = self.rows * 3 // 16
+        at, size = {
+            None: (0, self.rows), 0: (0, self.rows // 2), 1: (self.rows // 2, self.rows // 2),
+            2: (0, self.rows - short), 3: (self.rows - short, short),
+        }[half]
+        first = self.base + index * self.rows + at
+        return self.buf.at[pl.ds(pl.multiple_of(first, 16), size), :]
 
     def put(self, event, target, src, dst):
         copy = pltpu.make_async_remote_copy(
-            src_ref=src, dst_ref=dst, send_sem=self.send.at[event], recv_sem=self.recv.at[event],
+            src_ref=src, dst_ref=dst, send_sem=self.send, recv_sem=self.recv.at[event],
             device_id=target, device_id_type=MESH,
         )
         copy.start()
@@ -76,7 +80,7 @@
     def arrive(self, event, index, half=None):
         piece = self.slot(index, half)
         pltpu.make_async_remote_copy(
-            src_ref=piece, dst_ref=piece, send_sem=self.send.at[event],
+            src_ref=piece, dst_ref=piece, send_sem=self.send,
             recv_sem=self.recv.at[event], device_id=self.sib, device_id_type=MESH,
         ).wait_recv()
 
@@ -91,16 +95,18 @@
         at = self.at
         index = at.ctx_at(flip_col=True)
         self.arrive(1, index)
-        self.pass_on(4, self.up, index)
-        self.pass_on(5, self.down, index)
+        self.pass_on(4, self.up, index, 2)
+        self.pass_on(5, self.down, index, 2)
         self.pass_on(9, self.sib, index)
         index = at.ctx_at(dz=-1)
         self.arrive(2, index)
         self.pass_on(6, self.up, index, 0)
+        self.pass_on(16, self.xn, index, 3)
         self.pass_on(10, self.sib, index)
         index = at.ctx_at(dz=1)
         self.arrive(3, index)
         self.pass_on(7, self.down, index, 1)
+        self.pass_on(17, self.xn, index, 3)
         self.pass_on(11, self.sib, index)
 
     def third(self):
@@ -112,7 +118,8 @@
         self.pass_on(14, self.sib, index)
         for event, dz, on in ((4, -1, 12), (5, 1, 13)):
             index = at.ctx_at(flip_col=True, dz=dz)
-            self.arrive(event, index)
+            self.arrive(event, index, 2)
+            self.arrive(event + 12, index, 3)
             self.pass_on(on, self.sib, index)
 
     def last(self):
@@ -121,24 +128,26 @@
         self.arrive(8, index)
         self.pass_on(15, self.sib, index)
 
+    def from_core(self, pieces):
+        for event, flip_col, dz in pieces:
+            self.arrive(event, self.at.ctx_at(flip_col=flip_col, dz=dz, flip_core=True))
+
+    def near(self):
+        self.from_core(((0, False, 0), (10, False, -1), (12, True, -1)))
+
+    def rest(self):
+        self.from_core(((9, True, 0), (11, False, 1), (13, True, 1), (14, False, 2), (15, True, 2)))
+
     def whole(self):
-        at = self.at
-        for event, flip_col, dz in (
-            (0, False, 0), (9, True, 0), (10, False, -1), (11, False, 1),
-            (12, True, -1), (13, True, 1), (14, False, 2), (15, True, 2),
-        ):
-            self.arrive(event, at.ctx_at(flip_col=flip_col, dz=dz, flip_core=True))
-
-    halves = (6, 7)
-    events = 16
+        self.near()
+        self.rest()
 
     def close(self):
-        for event in range(self.events):
-            piece = self.slot(0, 0 if event in self.halves else None)
-            pltpu.make_async_remote_copy(
-                src_ref=piece, dst_ref=piece, send_sem=self.send.at[event],
-                recv_sem=self.recv.at[event], device_id=self.sib, device_id_type=MESH,
-            ).wait_send()
+        sent = self.buf.at[pl.ds(self.base, 15 * self.rows), :]
+        pltpu.make_async_remote_copy(
+            src_ref=sent, dst_ref=sent, send_sem=self.send, recv_sem=self.recv.at[0],
+            device_id=self.sib, device_id_type=MESH,
+        ).wait_send()
 
 
 class Features:
@@ -159,7 +168,7 @@
     def arrive(self, event, index, half=None):
         piece = self.slot(index, half)
         pltpu.make_async_remote_copy(
-            src_ref=piece, dst_ref=piece, send_sem=self.send.at[event],
+            src_ref=piece, dst_ref=piece, send_sem=self.send,
             recv_sem=self.recv.at[event], device_id=self.partner, device_id_type=MESH,
         ).wait_recv()
 
@@ -198,9 +207,12 @@
             self.arrive(event, index, 0)
             self.arrive(event + 1, index, 1)
 
-    halves = (5, 6, 7, 8)
-    events = 9
-    close = Gather.close
+    def close(self):
+        sent = self.buf.at[:, : 7 * 512]
+        pltpu.make_async_remote_copy(
+            src_ref=sent, dst_ref=sent, send_sem=self.send, recv_sem=self.recv.at[0],
+            device_id=self.partner, device_id_type=MESH,
+        ).wait_send()
 
 
 def dot_nt(left, right):
@@ -232,7 +244,7 @@
     def gather(t, own, buf, rows, base=0):
         return Gather(at, own, buf, rows, send.at[t], recv.at[t], base)
 
-    feats = Features(at, x_ref, x_buf, x_send, x_recv)
+    feats = Features(at, x_ref, x_buf, x_send.at[0], x_recv)
     wk = gather(0, wk_ref, w_buf, ROWS)
     wv = gather(1, wv_ref, wv_buf, ROWS)
     wq = gather(2, wq_ref, w_buf, ROWS, TOKENS)
@@ -275,8 +287,8 @@
         copy.wait()
 
     wk.second()
+    wq.first()
     feats.second()
-    wq.first()
     wk.third()
     feats.third()
     wq.second()
@@ -327,33 +339,7 @@
     keep(1, project(wv_buf), values.slot(at.ctx))
     values.first()
     wo.second()
-    keys.whole()
-
-    steps = {2: [values.second], 5: [wo.third]}
-
-    def block_logits(b, _):
-        for when, actions in steps.items():
-
-            @pl.when(b == when)
-            def _(actions=actions):
-                for action in actions:
-                    action()
-
-        @pl.when(b < blocks)
-        def _():
-            for h in range(GROUP):
-                rows = k_buf[pl.ds(pl.multiple_of(HD - 16 + b * KB, 16), KB + 32), h * HD : (h + 1) * HD]
-                k32[h] = rows.astype(jnp.float32)
-                for c in range(CK):
-                    start = 16 + CK // 2 - c
-                    kc[h % 2, :, c * HD : (c + 1) * HD] = k32[h, start : start + KB].astype(jnp.bfloat16)
-                lg[h, :, pl.ds(pl.multiple_of(HD + b * KB, HD), KB)] = dot_nt(qt[h], kc[h % 2])
-
-        return 0
-
-    lax.fori_loop(0, 8, block_logits, 0)
-    values.third()
-
+    keys.near()
     for s in range(2):
         for h in range(GROUP):
             cols = slice(h * HD, (h + 1) * HD)
@@ -368,9 +354,6 @@
             band[s * GROUP + h, 0] = kept[:, :HD]
             band[s * GROUP + h, 1] = kept[:, HD:]
 
-    row_in = lax.broadcasted_iota(jnp.int32, (8, HD), 0)
-    col_in = lax.broadcasted_iota(jnp.int32, (8, HD), 1)
-
     def taps(h, lags, width):
         total = None
         for c in range(CK):
@@ -383,9 +366,8 @@
         return total
 
     def two_tiles(k, _):
+        rows = pl.ds(pl.multiple_of(8 * k, 8), 8)
         for s in range(2):
-            here_cols = pl.ds(pl.multiple_of(HD + r0 + s * HD, HD), HD)
-            prior = pl.ds(pl.multiple_of(r0 + s * HD, HD), HD)
             for h in range(GROUP):
                 views = [
                     band.at[s * GROUP + h, t, pl.ds(pl.multiple_of(8 * k, 8), 16)] for t in range(2)
@@ -394,35 +376,69 @@
                     jnp.concatenate([view[8 - a : 16 - a] for view in views], 1) for a in range(CQ)
                 ]
                 direct = taps(h, lags, 2 * HD)
-                rows = pl.ds(pl.multiple_of(s * HD + 8 * k, 8), 8)
-                apart = 8 * k + row_in - col_in
-                lg[h, rows, prior] = jnp.where(
-                    apart + HD >= BAND, lg[h, rows, prior], direct[:, :HD]
-                )
-                lg[h, rows, here_cols] = jnp.where(
-                    apart >= BAND,
-                    lg[h, rows, here_cols],
-                    jnp.where(apart >= 0, direct[:, HD:], -jnp.inf),
-                )
+                band[s * GROUP + h, 0, rows] = direct[:, :HD]
+                band[s * GROUP + h, 1, rows] = direct[:, HD:]
         return 0
 
     def one_tile(k, _):
+        rows = pl.ds(pl.multiple_of(8 * k, 8), 8)
         for s in range(2):
-            here_cols = pl.ds(pl.multiple_of(HD + r0 + s * HD, HD), HD)
             for h in range(GROUP):
                 view = band.at[s * GROUP + h, 1, pl.ds(pl.multiple_of(8 * k, 8), 16)]
-                direct = taps(h, [view[8 - a : 16 - a] for a in range(CQ)], HD)
-                rows = pl.ds(pl.multiple_of(s * HD + 8 * k, 8), 8)
-                apart = 8 * k + row_in - col_in
-                lg[h, rows, here_cols] = jnp.where(
-                    apart >= BAND,
-                    lg[h, rows, here_cols],
-                    jnp.where(apart >= 0, direct, -jnp.inf),
-                )
+                band[s * GROUP + h, 1, rows] = taps(h, [view[8 - a : 16 - a] for a in range(CQ)], HD)
         return 0
 
     lax.fori_loop(0, 2, two_tiles, 0)
     lax.fori_loop(2, HD // 8, one_tile, 0)
+    keys.rest()
+
+    steps = {2: [values.second], 5: [wo.third]}
+
+    def block_logits(b, _):
+        for when, actions in steps.items():
+
+            @pl.when(b == when)
+            def _(actions=actions):
+                for action in actions:
+                    action()
+
+        @pl.when(b < blocks)
+        def _():
+            for h in range(GROUP):
+                rows = k_buf[pl.ds(pl.multiple_of(HD - 16 + b * KB, 16), KB + 32), h * HD : (h + 1) * HD]
+                k32[h] = rows.astype(jnp.float32)
+                for c in range(CK):
+                    start = 16 + CK // 2 - c
+                    kc[h % 2, :, c * HD : (c + 1) * HD] = k32[h, start : start + KB].astype(jnp.bfloat16)
+                logits = dot_nt(qt[h], kc[h % 2])
+                lg[h, :, pl.ds(pl.multiple_of(HD + b * KB, HD), KB)] = logits
+                peak = logits[:, :HD]
+                for t in range(1, KB // HD):
+                    peak = jnp.maximum(peak, logits[:, t * HD : (t + 1) * HD])
+                peaks[h] = jnp.maximum(peaks[h], jnp.where(b < blocks - 2, peak, -jnp.inf))
+
+        return 0
+
+    peaks[...] = jnp.full_like(peaks, -jnp.inf)
+    lax.fori_loop(0, 8, block_logits, 0)
+    values.third()
+
+    apart = lax.broadcasted_iota(jnp.int32, (HD, HD), 0) - lax.broadcasted_iota(jnp.int32, (HD, HD), 1)
+    for s in range(2):
+        here_cols = pl.ds(pl.multiple_of(HD + r0 + s * HD, HD), HD)
+        prior = pl.ds(pl.multiple_of(r0 + s * HD, HD), HD)
+        for h in range(GROUP):
+            rows = slice(s * HD, (s + 1) * HD)
+            lg[h, rows, here_cols] = jnp.where(
+                apart >= BAND,
+                lg[h, rows, here_cols],
+                jnp.where(apart >= 0, band[s * GROUP + h, 1, :HD], -jnp.inf),
+            )
+            rows = slice(s * HD, s * HD + 16)
+            lg[h, rows, prior] = jnp.where(
+                apart[:16] + HD >= BAND, lg[h, rows, prior], band[s * GROUP + h, 0, :16]
+            )
+
     for h in range(GROUP):
         lg[h, :HD, pl.ds(pl.multiple_of(2 * HD + r0, HD), HD)] = jnp.full(
             (HD, HD), -jnp.inf, jnp.float32
@@ -444,7 +460,7 @@
                 peak = jnp.maximum(peak, block[:, t * HD : (t + 1) * HD])
             return peak
 
-        peak = lax.fori_loop(0, blocks, peak_of, jnp.full((ROWS, HD), -jnp.inf, jnp.float32))
+        peak = lax.fori_loop(jnp.maximum(blocks - 2, 0), blocks, peak_of, peaks[g])
         peaks[g] = jnp.broadcast_to(jnp.max(peak, axis=1, keepdims=True), (ROWS, HD))
 
     wk.close()
@@ -611,7 +627,7 @@
             half(4, 2, ROWS, width),
             half(4, 2, 2, ROWS // 8, width), half(4, 2, 2, ROWS // 4, width), half(4, 2, 2, ROWS // 4, width),
             half(4, ROWS // 4, width), half(4, ROWS // 4, width),
-            dma((6, 16)), dma((6, 16)), dma((9,)), dma((9,)), dma((8,)), dma((2,)), dma((4, 5)), dma((4, 5)),
+            dma((6,)), dma((6, 18)), dma((1,)), dma((9,)), dma((8,)), dma((2,)), dma((4, 5)), dma((4, 5)),
         ],
         compiler_params=pltpu.CompilerParams(
             collective_id=1, has_side_effects=True, vmem_limit_bytes=67043328

time: 145 us -> 139 us (0.959)
  Pallas kernels: 142 us -> 135 us
    pallas_call x1, Pallas kernels: 142 us -> 135 us  [layer(): pl.pallas_call(layer_kernel, out_shape=jax.ShapeDtypeStruct((ROWS, width)...]
where the time goes in v6:
time: 139 us
  Pallas kernels  135 us (97%)
  local copies, waits for them, and re-layouts  2.34 us (2%)
  other arithmetic  1.4 us (1%)
    pallas_call x1, Pallas kernels, layer(): pl.pallas_call(layer_kernel, out_shape=jax.ShapeDtypeStruct((ROWS, width)...  135 us

profile of v6, /device:TPU:98, one launch (start us, length us, event | category | flops | bytes accessed | tf_op | source)
XLA Modules:
  0.0 139.0 jit_solution(7686510473157304903)
XLA Ops:
  0.0 0.0 copy-start
  0.0 0.7 copy-done
  0.7 0.5 fusion
  1.2 0.9 pad_maximum_fusion
  2.1 135.2 %layer.1 = bf16[256,512]{1,0:T(8,128)(2,1)} custom-call(bf16[256,512]{1,0:T(8,128)(2,1)} %x_ref.1, bf16[256,512]{1,0:T(8,128)(2,1)} %wk_ref.1, bf16[256,512]{1,0:T(8,128)(2,1)} %wv_ref.1, bf16[256,512]{1,0:T(8,128)(2,1)} %wq_ref.1, bf16[512,256]{1,0:T(8,128)(2,1)} %wo_ref.1, f32[4,66]{1,0:T(4,128)} %kern_ref.1, f32[4,4]{1,0:T(4,128)} %mix_ref.1, ...), custom_call_target="tpu_custom_call" | custom-call | tf_op jit(solution)/shard_map/layer/pallas_call | solution.py:613
  137.3 1.7 %copy.11 = bf16[256,512]{1,0:T(8,128)(2,1)} copy(bf16[256,512]{1,0:T(8,128)(2,1)} %layer.1) | data formatting | bytes 524288
  (2 shorter events, 0.0 us)
Async XLA Ops:
  0.0 0.7 copy-start

commit v7 on v6

--- a/solution.py
+++ b/solution.py
@@ -222,8 +222,8 @@
 
 
 def layer_kernel(
-    x_ref, wk_ref, wv_ref, wq_ref, wo_ref, kern_ref, mix_ref, cos_ref, sin_ref, gain_ref, o_ref,
-    x_buf, w_buf, wv_buf, k_buf, v_buf, wo_buf, made, qx, rim_in,
+    x_ref, wk_ref, wv_ref, wq_ref, wo_ref, kern_ref, mix_ref, pos_ref, gain_ref, o_ref,
+    cos_ref, sin_ref, x_buf, w_buf, wv_buf, k_buf, v_buf, wo_buf, made, qx, rim_in,
     q32, k32, qt, kc, lg, band, acc, mass, peaks, normed, part,
     y_half, y_sum, y_full, give, got,
     send, recv, x_send, x_recv, here, rim_sems, r_send, r_recv,
@@ -269,6 +269,17 @@
     met()
     wk.first()
     feats.first()
+
+    lane = lax.broadcasted_iota(jnp.int32, (HD, HD), 1)
+    lower = lane < HD // 2
+    exponents = jnp.where(lower, lane, lane - HD // 2).astype(jnp.float32) * (2.0 / HD)
+    inverse_rate = jnp.exp(-exponents * math.log(500000.0))
+    for t in range(ROWS // HD):
+        along = jnp.broadcast_to(pos_ref[t : t + 1].astype(jnp.float32) * 0.25, (HD, HD))
+        angle = jnp.transpose(along) * inverse_rate
+        sine = jnp.sin(angle)
+        cos_ref[t * HD : (t + 1) * HD] = jnp.cos(angle)
+        sin_ref[t * HD : (t + 1) * HD] = jnp.where(lower, -sine, sine)
 
     def project(buf):
         return jnp.dot(x_buf[...], buf[:TOKENS], preferred_element_type=jnp.float32)
@@ -613,9 +624,10 @@
     return pl.pallas_call(
         layer_kernel,
         out_shape=jax.ShapeDtypeStruct((ROWS, width), jnp.bfloat16),
-        in_specs=[hbm] * 5 + [smem] * 2 + [vmem] * 3,
+        in_specs=[hbm] * 5 + [smem] * 2 + [vmem] * 2,
         out_specs=vmem,
         scratch_shapes=[
+            full(ROWS, HD), full(ROWS, HD),
             half(ROWS, TOKENS), half(2 * TOKENS, width), half(TOKENS, width),
             half(HD + TOKENS + 16, width), half(TOKENS, width), half(16 * width, ROWS),
             half(3, ROWS, width), half(ROWS + 16, width), half(16, width),
@@ -639,15 +651,9 @@
 def per_device(
     activations, positions, w_query, w_key, w_value, conv_kernel, head_mix, out_gain, w_out
 ):
-    exponents = jnp.arange(HD // 2, dtype=jnp.float32) * (2.0 / HD)
-    inverse = jnp.exp(-exponents * math.log(500000.0))
-    angle = (positions.astype(jnp.float32) * 0.25)[:, None] * inverse[None, :]
-    cosine = jnp.cos(angle)
-    sine = jnp.sin(angle)
     return layer(
         activations, w_key, w_value, w_query, w_out, conv_kernel, head_mix,
-        jnp.concatenate([cosine, cosine], 1), jnp.concatenate([-sine, sine], 1),
-        out_gain.reshape(1, -1),
+        positions.reshape(ROWS // HD, HD), out_gain.reshape(1, -1),
     )
 
 

time: 139 us -> 137 us (0.986)
  other arithmetic: 1.4 us -> 0 us
where the time goes in v7:
time: 137 us
  Pallas kernels  135 us (99%)
  local copies, waits for them, and re-layouts  1.67 us (1%)
    pallas_call x1, Pallas kernels, layer(): pl.pallas_call(layer_kernel, out_shape=jax.ShapeDtypeStruct((ROWS, width)...  135 us

profile of v7, /device:TPU:98, one launch (start us, length us, event | category | flops | bytes accessed | tf_op | source)
XLA Modules:
  0.0 136.7 jit_solution(2878314587273837836)
XLA Ops:
  0.0 135.0 %layer.1 = bf16[256,512]{1,0:T(8,128)(2,1)} custom-call(bf16[256,512]{1,0:T(8,128)(2,1)} %x_ref.1, bf16[256,512]{1,0:T(8,128)(2,1)} %wk_ref.1, bf16[256,512]{1,0:T(8,128)(2,1)} %wv_ref.1, bf16[256,512]{1,0:T(8,128)(2,1)} %wq_ref.1, bf16[512,256]{1,0:T(8,128)(2,1)} %wo_ref.1, f32[4,66]{1,0:T(4,128)} %kern_ref.1, f32[4,4]{1,0:T(4,128)} %mix_ref.1, ...), custom_call_target="tpu_custom_call" | custom-call | tf_op jit(solution)/shard_map/layer/pallas_call | solution.py:624
  135.0 1.7 %copy.11 = bf16[256,512]{1,0:T(8,128)(2,1)} copy(bf16[256,512]{1,0:T(8,128)(2,1)} %layer.1) | data formatting | bytes 524288

commit v8 on v7

--- a/solution.py
+++ b/solution.py
@@ -403,7 +403,7 @@
     lax.fori_loop(2, HD // 8, one_tile, 0)
     keys.rest()
 
-    steps = {2: [values.second], 5: [wo.third]}
+    steps = {2: [values.second], 4: [wo.third], 7: [values.third]}
 
     def block_logits(b, _):
         for when, actions in steps.items():
@@ -432,7 +432,6 @@
 
     peaks[...] = jnp.full_like(peaks, -jnp.inf)
     lax.fori_loop(0, 8, block_logits, 0)
-    values.third()
 
     apart = lax.broadcasted_iota(jnp.int32, (HD, HD), 0) - lax.broadcasted_iota(jnp.int32, (HD, HD), 1)
     for s in range(2):
@@ -555,27 +554,27 @@
         total = mine + got[r].astype(jnp.float32)
         o_ref[r * chunk : (r + 1) * chunk] = total.astype(jnp.bfloat16)
 
+    acc[...] = jnp.zeros_like(acc)
+
+    def weigh(b, _):
+        left = w_buf[pl.ds(pl.multiple_of(b * GROUP * ROWS, GROUP * ROWS), GROUP * ROWS)]
+        block = v_buf[pl.ds(pl.multiple_of(b * KB, KB), KB), :]
+        acc[...] += jnp.dot(left, block, preferred_element_type=jnp.float32)
+        return 0
+
+    lax.fori_loop(0, blocks, weigh, 0)
     for r in range(2):
         rows = slice(r * HALF, (r + 1) * HALF)
-        acc[...] = jnp.zeros_like(acc)
-
-        def weigh(b, _, r=r):
-            first = b * GROUP * ROWS + r * GROUP * HALF
-            left = w_buf[pl.ds(pl.multiple_of(first, HALF), GROUP * HALF)]
-            block = v_buf[pl.ds(pl.multiple_of(b * KB, KB), KB), :]
-            acc[...] += jnp.dot(left, block, preferred_element_type=jnp.float32)
-            return 0
-
-        lax.fori_loop(0, blocks, weigh, 0)
+        base = r * GROUP * HALF
         inverse = [
             jnp.broadcast_to(1.0 / jnp.sum(mass[g, rows], axis=1, keepdims=True), (HALF, HD))
             for g in range(GROUP)
         ]
         for h in range(GROUP):
             cols = slice(h * HD, (h + 1) * HD)
-            total = mix_ref[h, 0] * (acc[:HALF, cols] * inverse[0])
+            total = mix_ref[h, 0] * (acc[base : base + HALF, cols] * inverse[0])
             for g in range(1, GROUP):
-                total = total + mix_ref[h, g] * (acc[g * HALF : (g + 1) * HALF, cols] * inverse[g])
+                total = total + mix_ref[h, g] * (acc[base + g * HALF : base + (g + 1) * HALF, cols] * inverse[g])
             rms = jnp.sqrt(jnp.mean(total * total, axis=1, keepdims=True) + 1e-05)
             normed[rows, cols] = (total / rms * gain_ref[:, cols]).astype(jnp.bfloat16)
 
@@ -634,7 +633,7 @@
             full(GROUP, ROWS + 8, HD), full(GROUP, KB + 32, HD),
             half(GROUP, ROWS, CK * HD), half(2, KB, CK * HD),
             full(GROUP, ROWS, HD + TOKENS), full(2 * GROUP, 2, HD + 8, HD),
-            full(GROUP * HALF, width),
+            full(GROUP * ROWS, width),
             full(GROUP, ROWS, HD), full(GROUP, ROWS, HD), half(ROWS, width),
             half(4, 2, ROWS, width),
             half(4, 2, 2, ROWS // 8, width), half(4, 2, 2, ROWS // 4, width), half(4, 2, 2, ROWS // 4, width),

time: 137 us -> 135 us (0.985)
    pallas_call x1, Pallas kernels: 135 us -> 134 us  [layer(): pl.pallas_call(layer_kernel, out_shape=jax.ShapeDtypeStruct((ROWS, width)...]
where the time goes in v8:
time: 135 us
  Pallas kernels  134 us (99%)
  local copies, waits for them, and re-layouts  1.67 us (1%)
    pallas_call x1, Pallas kernels, layer(): pl.pallas_call(layer_kernel, out_shape=jax.ShapeDtypeStruct((ROWS, width)...  134 us

profile of v8, /device:TPU:98, one launch (start us, length us, event | category | flops | bytes accessed | tf_op | source)
XLA Modules:
  0.0 135.3 jit_solution(11343476741664745274)
XLA Ops:
  0.0 133.6 %layer.1 = bf16[256,512]{1,0:T(8,128)(2,1)} custom-call(bf16[256,512]{1,0:T(8,128)(2,1)} %x_ref.1, bf16[256,512]{1,0:T(8,128)(2,1)} %wk_ref.1, bf16[256,512]{1,0:T(8,128)(2,1)} %wv_ref.1, bf16[256,512]{1,0:T(8,128)(2,1)} %wq_ref.1, bf16[512,256]{1,0:T(8,128)(2,1)} %wo_ref.1, f32[4,66]{1,0:T(4,128)} %kern_ref.1, f32[4,4]{1,0:T(4,128)} %mix_ref.1, ...), custom_call_target="tpu_custom_call" | custom-call | tf_op jit(solution)/shard_map/layer/pallas_call | solution.py:623
  133.6 1.7 %copy.11 = bf16[256,512]{1,0:T(8,128)(2,1)} copy(bf16[256,512]{1,0:T(8,128)(2,1)} %layer.1) | data formatting | bytes 524288
